TPU v7x, 32 devices: a whole 2x2x4 slice. The times are simulated.
32 devices in a mesh: head: 2 (over x), seq: 16 (over z, y, core).
Axes of the slice: x: 2, y: 2, z: 4, core: 2. Of those that a mesh axis runs over, the one named last changes fastest.
Arguments:
- layer_input: bfloat16 [16, 1024, 1024], P('seq', 'head'), may hold values from -6 to 6
- segment_ids: int32 [16384], replicated, may hold values from 0 to 31, never falling along the last dimension, each value on 1 to 4096 neighbouring positions
- norm1_gain: bfloat16 [1024], P(('head', 'seq')), may hold values from 0.5 to 1.5
- w_query: bfloat16 [1024, 256], P(('head', 'seq')), may hold values from -0.1875 to 0.1875
- w_key: bfloat16 [1024, 256], P(('head', 'seq')), may hold values from -0.1875 to 0.1875
- w_value: bfloat16 [1024, 1024], P(('head', 'seq')), may hold values from -0.1875 to 0.1875
- w_out: bfloat16 [1024, 1024], P(('head', 'seq')), may hold values from -1.5 to 1.5
- norm2_gain: bfloat16 [1024], P(('head', 'seq')), may hold values from 0.5 to 1.5
- w_gate: bfloat16 [1024, 2752], P('seq', 'head'), may hold values from -0.1875 to 0.1875
- w_up: bfloat16 [1024, 2752], P('seq', 'head'), may hold values from -0.1875 to 0.1875
- w_down: bfloat16 [2752, 1024], P('head', 'seq'), may hold values from -0.109375 to 0.109375
- output_grad: bfloat16 [16, 1024, 1024], P('seq', 'head'), may hold values from -6 to 6
Outputs:
- layer_output: bfloat16 [16, 1024, 1024], P('seq', 'head')
- input_grad: float32 [16, 1024, 1024], P('seq', 'head')
- d_norm1_gain: float32 [1024], P(('head', 'seq'))
- d_w_query: float32 [1024, 256], P(('head', 'seq'))
- d_w_key: float32 [1024, 256], P(('head', 'seq'))
- d_w_value: float32 [1024, 1024], P(('head', 'seq'))
- d_w_out: float32 [1024, 1024], P(('head', 'seq'))
- d_norm2_gain: float32 [1024], P(('head', 'seq'))
- d_w_gate: float32 [1024, 2752], P('seq', 'head')
- d_w_up: float32 [1024, 2752], P('seq', 'head')
- d_w_down: float32 [2752, 1024], P('head', 'seq')
Inputs may be any that keep to these rules, and one draw needn't show every extreme that they name: `segment_ids`: document numbers never fall along the stream; each document has 1 to 4096 tokens and one has exactly 4096.
All inputs are finite; a program needn't handle non-finite values.
Results may differ from a plain program's by a relative error of at most 0.013.
Values may be sent and summed in bfloat16 or wider, within the bound.
A program may use at most 320 MiB of HBM per device.

v0:
```python
import jax
import jax.numpy as jnp
from jax import lax
from jax.sharding import PartitionSpec as P

HEADS = 16
QD = 16
VD = 64
DOC_MAX = 4096


EPSILON = 1e-05


def passed_along(block, axis, distance):
    devices = range(lax.axis_size(axis))
    route = [(i - distance, i) for i in devices if i - distance in devices]
    return lax.ppermute(block, axis, route)


def rms_scale(values, gain):
    return values * lax.rsqrt(jnp.mean(values * values, axis=-1, keepdims=True) + EPSILON) * gain


def swish_mix(gate, up_proj):
    return jax.nn.silu(gate) * up_proj


def times_left(left, right):
    return lax.dot_general(
        left, right, (((0,), (0,)), ((), ())), preferred_element_type=jnp.float32
    )


def times_right(left, right):
    return lax.dot_general(
        left, right, (((1,), (1,)), ((), ())), preferred_element_type=jnp.float32
    )


def pair_scores(query_heads, key_heads, query_ids, key_ids, causal):
    scores = jnp.einsum(
        "qhd,khd->hqk", query_heads, key_heads, preferred_element_type=jnp.float32
    ) * QD ** (-0.5)
    visible = query_ids[:, None] == key_ids[None, :]
    if causal:
        rows_here = query_heads.shape[0]
        lower = lax.broadcasted_iota(jnp.int32, (rows_here, rows_here), 1) <= lax.broadcasted_iota(
            jnp.int32, (rows_here, rows_here), 0
        )
        visible = visible & lower
    weights = jnp.where(visible[None], 1.0 + scores + 0.5 * scores * scores, 0.0)
    return (scores, visible, weights)


def pair_forward(query_heads, key_heads, value_heads, query_ids, key_ids, causal):
    scores, visible, weights = pair_scores(query_heads, key_heads, query_ids, key_ids, causal)
    numerator = jnp.einsum(
        "hqk,khd->qhd",
        weights.astype(jnp.bfloat16),
        value_heads,
        preferred_element_type=jnp.float32,
    )
    return (numerator, jnp.sum(weights, axis=2).T)


def pair_backward(
    query_heads, key_heads, value_heads, query_ids, key_ids, causal, grad_numerator, delta
):
    scores, visible, weights = pair_scores(query_heads, key_heads, query_ids, key_ids, causal)
    grad_prob = jnp.einsum(
        "qhd,khd->hqk", grad_numerator, value_heads, preferred_element_type=jnp.float32
    )
    grad_scores = jnp.where(
        visible[None], (grad_prob - delta.T[:, :, None]) * (1.0 + scores), 0.0
    ).astype(jnp.bfloat16)
    scale = QD ** (-0.5)
    grad_query = (
        jnp.einsum("hqk,khd->qhd", grad_scores, key_heads, preferred_element_type=jnp.float32)
        * scale
    )
    grad_key = (
        jnp.einsum("hqk,qhd->khd", grad_scores, query_heads, preferred_element_type=jnp.float32)
        * scale
    )
    grad_value = jnp.einsum(
        "hqk,qhd->khd",
        weights.astype(jnp.bfloat16),
        grad_numerator,
        preferred_element_type=jnp.float32,
    )
    return (grad_query, grad_key, grad_value)


def body(
    layer_input,
    segment_ids,
    norm1_gain,
    w_query,
    w_key,
    w_value,
    w_out,
    norm2_gain,
    w_gate,
    w_up,
    w_down,
    output_grad,
):
    tok_rows = layer_input.shape[1]
    groups = lax.axis_size("head")
    seg_rows = tok_rows * groups
    reach = DOC_MAX // seg_rows
    local_heads = HEADS // groups
    seq_pos = lax.axis_index("seq")
    query_ids = lax.dynamic_slice_in_dim(segment_ids, seq_pos * seg_rows, seg_rows)

    def earlier_ids(step):
        key_start = jnp.maximum(seq_pos - step, 0) * seg_rows
        key_ids = lax.dynamic_slice_in_dim(segment_ids, key_start, seg_rows)
        needed = (seq_pos >= step) & (key_ids[seg_rows - 1] == query_ids[0])
        return (key_ids, needed)

    gain_one, query_full, key_full, value_full, out_full, gain_two = (
        lax.all_gather(norm1_gain, ("head", "seq"), axis=0, tiled=True),
        lax.all_gather(w_query, ("head", "seq"), axis=0, tiled=True),
        lax.all_gather(w_key, ("head", "seq"), axis=0, tiled=True),
        lax.all_gather(w_value, ("head", "seq"), axis=0, tiled=True),
        lax.all_gather(w_out, ("head", "seq"), axis=0, tiled=True),
        lax.all_gather(norm2_gain, ("head", "seq"), axis=0, tiled=True),
    )
    gate_half, up_half, down_half = (
        lax.all_gather(w_gate, "seq", axis=0, tiled=True),
        lax.all_gather(w_up, "seq", axis=0, tiled=True),
        lax.all_gather(w_down, "seq", axis=1, tiled=True),
    )
    gate_used, up_used, down_used = (
        lax.all_gather(gate_half, "head", axis=1, tiled=True),
        lax.all_gather(up_half, "head", axis=1, tiled=True),
        lax.all_gather(down_half, "head", axis=0, tiled=True),
    )
    inputs = layer_input[0].astype(jnp.float32)
    gain_first = gain_one.astype(jnp.float32)
    gain_second = gain_two.astype(jnp.float32)
    normed_one = rms_scale(inputs, gain_first).astype(jnp.bfloat16)
    query_tok = jnp.dot(normed_one, query_full, preferred_element_type=jnp.float32).astype(
        jnp.bfloat16
    )
    key_tok = jnp.dot(normed_one, key_full, preferred_element_type=jnp.float32).astype(jnp.bfloat16)
    value_tok = jnp.dot(normed_one, value_full, preferred_element_type=jnp.float32).astype(
        jnp.bfloat16
    )
    query_seg, key_seg, value_seg = (
        lax.all_to_all(query_tok, "head", split_axis=1, concat_axis=0, tiled=True),
        lax.all_to_all(key_tok, "head", split_axis=1, concat_axis=0, tiled=True),
        lax.all_to_all(value_tok, "head", split_axis=1, concat_axis=0, tiled=True),
    )
    query_heads = query_seg.reshape(seg_rows, local_heads, QD)
    key_heads = key_seg.reshape(seg_rows, local_heads, QD)
    value_heads = value_seg.reshape(seg_rows, local_heads, VD)
    numerator, denominator = pair_forward(
        query_heads, key_heads, value_heads, query_ids, query_ids, True
    )

    def remote_forward(operands):
        key_block, value_block, key_ids = operands
        return pair_forward(
            query_heads,
            key_block.reshape(seg_rows, local_heads, QD),
            value_block.reshape(seg_rows, local_heads, VD),
            query_ids,
            key_ids,
            False,
        )

    def empty_forward(operands):
        return (jnp.zeros_like(numerator), jnp.zeros_like(denominator))

    kept = []
    key_now, value_now = (key_seg, value_seg)
    for step in range(1, reach + 1):
        key_now, value_now = passed_along((key_now, value_now), "seq", 1)
        kept.append((key_now, value_now))
        key_ids, needed = earlier_ids(step)
        extra_numerator, extra_denominator = lax.cond(
            needed, remote_forward, empty_forward, (key_now, value_now, key_ids)
        )
        numerator = numerator + extra_numerator
        denominator = denominator + extra_denominator
    attended = numerator / denominator[:, :, None]
    attended_seg = attended.astype(jnp.bfloat16).reshape(seg_rows, local_heads * VD)
    attended_tok = lax.all_to_all(attended_seg, "head", split_axis=0, concat_axis=1, tiled=True)
    residual = inputs + jnp.dot(attended_tok, out_full, preferred_element_type=jnp.float32)
    normed_two = rms_scale(residual, gain_second).astype(jnp.bfloat16)
    gate = jnp.dot(normed_two, gate_used, preferred_element_type=jnp.float32)
    up_proj = jnp.dot(normed_two, up_used, preferred_element_type=jnp.float32)
    hidden = swish_mix(gate, up_proj).astype(jnp.bfloat16)
    partial_down = jnp.dot(hidden, down_used, preferred_element_type=jnp.float32)
    outcome = (residual + partial_down).astype(jnp.bfloat16)
    grad_output = output_grad[0]
    grad_hidden = times_right(grad_output, down_used)
    grad_wdown = times_left(hidden, grad_output)
    mixed_value, mix_pull = jax.vjp(swish_mix, gate, up_proj)
    grad_gate, grad_up = mix_pull(grad_hidden)
    grad_gate = grad_gate.astype(jnp.bfloat16)
    grad_up = grad_up.astype(jnp.bfloat16)
    grad_wgate = times_left(normed_two, grad_gate)
    grad_wup = times_left(normed_two, grad_up)
    grad_normed_two = times_right(grad_gate, gate_used) + times_right(grad_up, up_used)
    norm_value, norm_pull = jax.vjp(rms_scale, residual, gain_second)
    grad_resid_two, grad_gain_two = norm_pull(grad_normed_two)
    grad_middle = grad_output.astype(jnp.float32) + grad_resid_two
    grad_middle_low = grad_middle.astype(jnp.bfloat16)
    grad_wout = times_left(attended_tok, grad_middle_low)
    grad_attended = times_right(grad_middle_low, out_full).astype(jnp.bfloat16)
    grad_att_seg = lax.all_to_all(grad_attended, "head", split_axis=1, concat_axis=0, tiled=True)
    grad_att_wide = grad_att_seg.reshape(seg_rows, local_heads, VD).astype(jnp.float32)
    grad_numerator = (grad_att_wide / denominator[:, :, None]).astype(jnp.bfloat16)
    delta = jnp.sum(grad_att_wide * attended, axis=2) / denominator
    grad_query, grad_key, grad_value = pair_backward(
        query_heads, key_heads, value_heads, query_ids, query_ids, True, grad_numerator, delta
    )

    def remote_backward(operands):
        key_block, value_block, key_ids = operands
        return pair_backward(
            query_heads,
            key_block.reshape(seg_rows, local_heads, QD),
            value_block.reshape(seg_rows, local_heads, VD),
            query_ids,
            key_ids,
            False,
            grad_numerator,
            delta,
        )

    def empty_backward(operands):
        return (jnp.zeros_like(grad_query), jnp.zeros_like(grad_key), jnp.zeros_like(grad_value))

    shifted = None
    for step in range(reach, 0, -1):
        key_block, value_block = kept[step - 1]
        key_ids, needed = earlier_ids(step)
        part_query, part_key, part_value = lax.cond(
            needed, remote_backward, empty_backward, (key_block, value_block, key_ids)
        )
        grad_query = grad_query + part_query
        if shifted is not None:
            part_key = part_key + shifted[0]
            part_value = part_value + shifted[1]
        shifted = (
            passed_along(part_key.astype(jnp.bfloat16), "seq", -1).astype(part_key.dtype),
            passed_along(part_value.astype(jnp.bfloat16), "seq", -1).astype(part_value.dtype),
        )
    grad_key = grad_key + shifted[0]
    grad_value = grad_value + shifted[1]
    grad_query_seg = grad_query.reshape(seg_rows, local_heads * QD).astype(jnp.bfloat16)
    grad_key_seg = grad_key.reshape(seg_rows, local_heads * QD).astype(jnp.bfloat16)
    grad_value_seg = grad_value.reshape(seg_rows, local_heads * VD).astype(jnp.bfloat16)
    grad_query_tok, grad_key_tok, grad_value_tok = (
        lax.all_to_all(grad_query_seg, "head", split_axis=0, concat_axis=1, tiled=True),
        lax.all_to_all(grad_key_seg, "head", split_axis=0, concat_axis=1, tiled=True),
        lax.all_to_all(grad_value_seg, "head", split_axis=0, concat_axis=1, tiled=True),
    )
    grad_wquery = times_left(normed_one, grad_query_tok)
    grad_wkey = times_left(normed_one, grad_key_tok)
    grad_wvalue = times_left(normed_one, grad_value_tok)
    grad_normed_one = (
        times_right(grad_query_tok, query_full)
        + times_right(grad_key_tok, key_full)
        + times_right(grad_value_tok, value_full)
    )
    first_value, first_pull = jax.vjp(rms_scale, inputs, gain_first)
    grad_inputs, grad_gain_one = first_pull(grad_normed_one)
    grad_layer = grad_middle + grad_inputs
    attn_shards = (
        lax.psum_scatter(grad_gain_one, ("head", "seq"), scatter_dimension=0, tiled=True),
        lax.psum_scatter(grad_wquery, ("head", "seq"), scatter_dimension=0, tiled=True),
        lax.psum_scatter(grad_wkey, ("head", "seq"), scatter_dimension=0, tiled=True),
        lax.psum_scatter(grad_wvalue, ("head", "seq"), scatter_dimension=0, tiled=True),
        lax.psum_scatter(grad_wout, ("head", "seq"), scatter_dimension=0, tiled=True),
        lax.psum_scatter(grad_gain_two, ("head", "seq"), scatter_dimension=0, tiled=True),
    )
    grad_wgate, grad_wup, grad_wdown = (
        lax.psum_scatter(
            grad_wgate.astype(jnp.bfloat16), "head", scatter_dimension=1, tiled=True
        ).astype(jnp.float32),
        lax.psum_scatter(
            grad_wup.astype(jnp.bfloat16), "head", scatter_dimension=1, tiled=True
        ).astype(jnp.float32),
        lax.psum_scatter(
            grad_wdown.astype(jnp.bfloat16), "head", scatter_dimension=0, tiled=True
        ).astype(jnp.float32),
    )
    ffn_shards = (
        lax.psum_scatter(grad_wgate, "seq", scatter_dimension=0, tiled=True),
        lax.psum_scatter(grad_wup, "seq", scatter_dimension=0, tiled=True),
        lax.psum_scatter(grad_wdown, "seq", scatter_dimension=1, tiled=True),
    )
    return (
        outcome[None],
        grad_layer[None],
        attn_shards[0],
        attn_shards[1],
        attn_shards[2],
        attn_shards[3],
        attn_shards[4],
        attn_shards[5],
        ffn_shards[0],
        ffn_shards[1],
        ffn_shards[2],
    )


def solution(mesh):
    in_specs = (
        P("seq", "head", None),
        P(),
        P(("head", "seq")),
        P(("head", "seq"), None),
        P(("head", "seq"), None),
        P(("head", "seq"), None),
        P(("head", "seq"), None),
        P(("head", "seq")),
        P("seq", "head"),
        P("seq", "head"),
        P("head", "seq"),
        P("seq", "head", None),
    )
    out_specs = (
        P("seq", "head", None),
        P("seq", "head", None),
        P(("head", "seq")),
        P(("head", "seq"), None),
        P(("head", "seq"), None),
        P(("head", "seq"), None),
        P(("head", "seq"), None),
        P(("head", "seq")),
        P("seq", "head"),
        P("seq", "head"),
        P("head", "seq"),
    )
    return jax.shard_map(body, mesh=mesh, in_specs=in_specs, out_specs=out_specs, check_vma=False)
```

profile of v0, /device:TPU:0, one launch (start us, length us, event | category | flops | bytes accessed | tf_op | source)
XLA Modules:
  0.0 1700.1 jit_solution(2689771494344564398)
XLA Ops:
  10.6 46.8 %all-gather.17.cloned.1.call-done = bf16[1024,1376]{1,0:T(8,128)(2,1)} async-done(((bf16[64,1376]{1,0:T(8,128)(2,1)}), bf16[1024,1376]{1,0:T(8,128)(2,1)}) %all-gather.17.cloned.1.call-update) | async-done | bytes 2818064 | tf_op jit(solution)/shard_map/all_gather | solution.py:133
  62.1 40.3 %all-gather.13.cloned.1.call-done = bf16[1024,1376]{1,0:T(8,128)(2,1)} async-done(((bf16[64,1376]{1,0:T(8,128)(2,1)}), bf16[1024,1376]{1,0:T(8,128)(2,1)}) %all-gather.13.cloned.1.call-update) | async-done | bytes 2818064 | tf_op jit(solution)/shard_map/all_gather | solution.py:132
  107.5 39.4 %all-reduce.5 = (bf16[1024]{0:T(1024)(128)(2,1)S(1)}, bf16[1024]{0:T(1024)(128)(2,1)}) all-reduce(bf16[1024]{0:T(1024)(128)(2,1)S(1)} %dynamic-update-slice, bf16[1024]{0:T(1024)(128)(2,1)S(1)} %dynamic-update-slice.1), channel_id=1, replica_groups=mesh['head'=2,'seq'=16] {'head','seq'}, use_global_device_ids=true, to_apply=%add | all-reduce | flops 2048 | bytes 8192
  147.3 12.8 all-gather.9.cloned.1.call-done
  163.1 16.7 all_to_all.134
  184.0 22.3 %collective-permute-start.3 = (bf16[1024,512]{0,1:T(8,128)(2,1)S(1)}, bf16[1024,512]{0,1:T(8,128)(2,1)}, u32[]{:S(2)}, u32[]{:S(2)}) collective-permute-start(bf16[1024,512]{0,1:T(8,128)(2,1)S(1)} %collective-permute-done.1), channel_id=1, source_target_pairs={{0,1},{1,2},{2,3},{3,4},{4,5},{5,6},{6,7},{7,8},{8,9},{9,10},{10,1... | collective-permute-start | bytes 3145736 | tf_op jit(solution)/shard_map/ppermute | solution.py:18
  206.2 46.8 %all_gather.39 = bf16[1024,256]{1,0:T(8,128)(2,1)S(1)} all-gather(bf16[32,256]{1,0:T(8,128)(2,1)S(1)} %copy-done.59), channel_id=1, replica_groups=mesh['head'=2,'seq'=16] {'head','seq'}, dimensions={0}, use_global_device_ids=true | all-gather | bytes 540672 | tf_op jit(solution)/shard_map/all_gather | solution.py:126
  261.4 41.0 %all_gather.38 = bf16[1024,256]{1,0:T(8,128)(2,1)S(1)} all-gather(bf16[32,256]{1,0:T(8,128)(2,1)S(1)} %copy-done.60), channel_id=1, replica_groups=mesh['head'=2,'seq'=16] {'head','seq'}, dimensions={0}, use_global_device_ids=true | all-gather | bytes 540672 | tf_op jit(solution)/shard_map/all_gather | solution.py:125
  333.7 20.0 %fusion.85 = (bf16[8,1024,1024]{1,2,0:T(8,128)(2,1)}, f32[8,1024]{1,0:T(8,128)}, f32[8,1024,1024]{1,2,0:T(8,128)}) fusion(pred[1024,1024]{0,1:T(8,128)(4,1)} %fusion.90, bf16[1024,8,16]{0,2,1:T(8,128)(2,1)S(1)} %reshape.464, bf16[1024,8,16]{0,2,1:T(8,128)(2,1)S(1)} %reshape.465), kind=kOutput, calls=%fused_computation.103 | convolution fusion | flops 335536128 | bytes 51937280 | tf_op jit(solution)/shard_map/qhd,khd->hqk/dot_general | solution.py:42
  359.9 11.5 fusion.143
  393.7 20.6 %all-to-all-done.3 = bf16[2,512,512]{1,2,0:T(8,128)(2,1)S(1)} async-done(((bf16[2,512,512]{1,2,0:T(8,128)(2,1)}), bf16[2,512,512]{1,2,0:T(8,128)(2,1)S(1)}, u32[]{:S(2)}, u32[]{:S(2)}) %all-to-all-start.3) | async-done | bytes 1048608 | tf_op jit(solution)/shard_map/all_to_all | solution.py:191
  439.1 62.2 %all-gather.23.cloned.1.call-done = bf16[2752,1024]{1,0:T(8,128)(2,1)} async-done(((bf16[1376,1024]{1,0:T(8,128)(2,1)}), bf16[2752,1024]{1,0:T(8,128)(2,1)}) %all-gather.23.cloned.1.call-update) | async-done | bytes 5636112 | tf_op jit(solution)/shard_map/all_gather | solution.py:139
  501.4 11.7 multiply_convert_fusion
  555.9 22.7 %all-to-all-done.4 = bf16[512,2,512]{0,2,1:T(8,128)(2,1)S(1)} async-done(((bf16[512,2,512]{0,2,1:T(8,128)(2,1)}), bf16[512,2,512]{0,2,1:T(8,128)(2,1)S(1)}, u32[]{:S(2)}, u32[]{:S(2)}) %all-to-all-start.4) | async-done | bytes 1048608 | tf_op jit(solution)/shard_map/all_to_all | solution.py:215
  595.6 17.4 %select_convert_fusion.20 = bf16[8,1024,1024]{1,2,0:T(8,128)(2,1)S(1)} fusion(f32[8,1024,1024]{1,2,0:T(8,128)} %get-tuple-element.269, f32[8,1024]{1,0:T(8,128)S(1)} %bitcast.305, pred[1024,1024]{0,1:T(8,128)(4,1)} %fusion.90, bf16[1024,8,64]{0,2,1:T(8,128)(2,1)} %get-tuple-element.263, bf16[1024,8,64]{0,2,1:T(8,128)(2,1)} %copy-done.14), kind=kOutput, calls=%fused_computation.100 | convolution fusion | flops 1124073472 | bytes 53510144 | tf_op jit(solution)/shard_map/qhd,khd->hqk/dot_general | solution.py:71
  629.0 10.3 conditional.14
  639.3 10.9 conditional.15
  658.9 40.9 %collective-permute-done.9 = bf16[1024,8,16]{0,2,1:T(8,128)(2,1)S(1)} collective-permute-done((bf16[1024,8,16]{0,2,1:T(8,128)(2,1)S(1)}, bf16[1024,8,16]{0,2,1:T(8,128)(2,1)S(1)}, u32[]{:S(2)}, u32[]{:S(2)}) %collective-permute-start.9) | collective-permute-done | bytes 262176 | tf_op jit(solution)/shard_map/ppermute | solution.py:18
  711.5 11.2 fusion.113
  722.9 10.8 all_to_all.135
  752.8 17.3 %collective-permute-done.13 = bf16[1024,8,64]{0,2,1:T(8,128)(2,1)S(1)} collective-permute-done((bf16[1024,8,64]{0,2,1:T(8,128)(2,1)S(1)}, bf16[1024,8,64]{0,2,1:T(8,128)(2,1)S(1)}, u32[]{:S(2)}, u32[]{:S(2)}) %collective-permute-start.13) | collective-permute-done | bytes 1048608 | tf_op jit(solution)/shard_map/ppermute | solution.py:18
  773.4 14.8 collective-permute-done.14
  792.6 11.3 fusion.148
  803.9 28.8 %collective-permute-done.15 = bf16[1024,8,64]{0,2,1:T(8,128)(2,1)} collective-permute-done((bf16[1024,8,64]{0,2,1:T(8,128)(2,1)}, bf16[1024,8,64]{0,2,1:T(8,128)(2,1)}, u32[]{:S(2)}, u32[]{:S(2)}) %collective-permute-start.15) | collective-permute-done | bytes 1048608 | tf_op jit(solution)/shard_map/ppermute | solution.py:18
  837.3 11.8 all_to_all.136
  881.7 201.4 %all-reduce.4 = (f32[1024]{0:T(1024)S(1)}, f32[1024]{0:T(1024)S(1)}) all-reduce(f32[1024]{0:T(1024)S(1)} %get-tuple-element.241, f32[1024]{0:T(1024)S(1)} %copy-done.58), channel_id=2, replica_groups=mesh['head'=2,'seq'=16] {'head','seq'}, use_global_device_ids=true, to_apply=%region_27.28.clone | all-reduce | flops 2048 | bytes 16384
  1087.7 70.8 %reduce-scatter.19.cloned.1.call-done = f32[32,256]{1,0:T(8,128)} async-done(((f32[1024,256]{1,0:T(8,128)}), f32[32,256]{1,0:T(8,128)}) %reduce-scatter.19.cloned.1.call-update) | async-done | bytes 32784 | tf_op jit(solution)/shard_map/reduce_scatter | solution.py:278
  1158.6 140.4 %reduce-scatter.23.cloned.1.call-done = f32[32,1024]{1,0:T(8,128)} async-done(((f32[1024,1024]{1,0:T(8,128)}), f32[32,1024]{1,0:T(8,128)}) %reduce-scatter.23.cloned.1.call-update) | async-done | bytes 131088 | tf_op jit(solution)/shard_map/reduce_scatter | solution.py:280
  1298.9 140.0 %reduce-scatter.21.cloned.1.call-done = f32[32,1024]{1,0:T(8,128)} async-done(((f32[1024,1024]{1,0:T(8,128)}), f32[32,1024]{1,0:T(8,128)}) %reduce-scatter.21.cloned.1.call-update) | async-done | bytes 131088 | tf_op jit(solution)/shard_map/reduce_scatter | solution.py:279
  1438.9 82.9 %reduce-scatter.31.cloned.1.call-done = f32[64,1376]{1,0:T(8,128)} async-done(((f32[1024,1376]{1,0:T(8,128)}), f32[64,1376]{1,0:T(8,128)}) %reduce-scatter.31.cloned.1.call-update) | async-done | bytes 352272
  1521.8 85.6 %reduce-scatter.33.cloned.1.call-done = f32[64,1376]{1,0:T(8,128)} async-done(((f32[1024,1376]{1,0:T(8,128)}), f32[64,1376]{1,0:T(8,128)}) %reduce-scatter.33.cloned.1.call-update) | async-done | bytes 352272
  1607.4 85.6 %reduce-scatter.35.cloned.1.call-done = f32[64,1376]{1,0:T(8,128)} async-done(((f32[1024,1376]{1,0:T(8,128)}), f32[64,1376]{1,0:T(8,128)}) %reduce-scatter.35.cloned.1.call-update) | async-done | bytes 352272
  (316 shorter events, 285.3 us)
Async XLA Ops:
  7.2 50.2 %all-gather.17.cloned.1.call-start = ((), (), s32[]{:S(2)}) async-start(), calls=%async_computation.22 | async-start | bytes 3063808 | tf_op jit(solution)/shard_map/all_gather | solution.py:133
  7.9 94.5 %all-gather.13.cloned.1.call-start = ((), (), s32[]{:S(2)}) async-start(), calls=%async_computation.20 | async-start | bytes 3063808 | tf_op jit(solution)/shard_map/all_gather | solution.py:132
  8.7 151.5 %all-gather.9.cloned.1.call-start = ((), (), s32[]{:S(2)}) async-start(), calls=%async_computation.18 | async-start | bytes 2162688 | tf_op jit(solution)/shard_map/all_gather | solution.py:127
  9.4 317.2 %all-gather.21.cloned.1.call-start = ((), (), s32[]{:S(2)}) async-start(), calls=%async_computation.24 | async-start | bytes 3063808 | tf_op jit(solution)/shard_map/all_gather | solution.py:134
  10.0 383.7 %all-gather.11.cloned.1.call-start = ((), (), s32[]{:S(2)}) async-start(), calls=%async_computation.19 | async-start | bytes 2162688 | tf_op jit(solution)/shard_map/all_gather | solution.py:128
  10.6 409.7 %all-gather.19.cloned.1.call-start = ((), (), s32[]{:S(2)}) async-start(), calls=%async_computation.23 | async-start | bytes 8454144 | tf_op jit(solution)/shard_map/all_gather | solution.py:138
  62.1 368.3 %all-gather.15.cloned.1.call-start = ((), (), s32[]{:S(2)}) async-start(), calls=%async_computation.21 | async-start | bytes 8454144 | tf_op jit(solution)/shard_map/all_gather | solution.py:137
  184.0 69.1 %collective-permute-start.3 = (bf16[1024,512]{0,1:T(8,128)(2,1)S(1)}, bf16[1024,512]{0,1:T(8,128)(2,1)}, u32[]{:S(2)}, u32[]{:S(2)}) collective-permute-start(bf16[1024,512]{0,1:T(8,128)(2,1)S(1)} %collective-permute-done.1), channel_id=1, source_target_pairs={{0,1},{1,2},{2,3},{3,4},{4,5},{5,6},{6,7},{7,8},{8,9},{9,10},{10,1... | collective-permute-start | bytes 3145736 | tf_op jit(solution)/shard_map/ppermute | solution.py:18
  253.1 78.2 %collective-permute-start.5 = (bf16[1024,512]{0,1:T(8,128)(2,1)}, bf16[1024,512]{0,1:T(8,128)(2,1)}, u32[]{:S(2)}, u32[]{:S(2)}) collective-permute-start(bf16[1024,512]{0,1:T(8,128)(2,1)} %collective-permute-done.3), channel_id=1, source_target_pairs={{0,1},{1,2},{2,3},{3,4},{4,5},{5,6},{6,7},{7,8},{8,9},{9,10},{10,1... | collective-permute-start | bytes 3145736 | tf_op jit(solution)/shard_map/ppermute | solution.py:18
  257.5 45.0 %all-to-all-start.2 = ((bf16[512,2,128]{0,2,1:T(8,128)(2,1)}), bf16[512,2,128]{0,2,1:T(8,128)(2,1)S(1)}, u32[]{:S(2)}, u32[]{:S(2)}) async-start(bf16[512,2,128]{0,2,1:T(8,128)(2,1)} %bitcast.44), calls=%async_computation.2 | async-start | bytes 524288 | tf_op jit(solution)/shard_map/all_to_all | solution.py:154
  306.1 16.4 all-to-all-start.1
  309.5 191.8 %all-gather.23.cloned.1.call-start = ((), (), s32[]{:S(2)}) async-start(), calls=%async_computation.25 | async-start | bytes 8454144 | tf_op jit(solution)/shard_map/all_gather | solution.py:139
  323.4 30.3 %collective-permute-start.4 = (bf16[1024,128]{0,1:T(8,128)(2,1)S(1)}, bf16[1024,128]{0,1:T(8,128)(2,1)}, u32[]{:S(2)}, u32[]{:S(2)}) collective-permute-start(bf16[1024,128]{0,1:T(8,128)(2,1)S(1)} %collective-permute-done.2), channel_id=1, source_target_pairs={{0,1},{1,2},{2,3},{3,4},{4,5},{5,6},{6,7},{7,8},{8,9},{9,10},{10,1... | collective-permute-start | bytes 786440 | tf_op jit(solution)/shard_map/ppermute | solution.py:18
  331.3 43.7 %collective-permute-start.7 = (bf16[1024,512]{0,1:T(8,128)(2,1)}, bf16[1024,512]{0,1:T(8,128)(2,1)}, u32[]{:S(2)}, u32[]{:S(2)}) collective-permute-start(bf16[1024,512]{0,1:T(8,128)(2,1)} %collective-permute-done.5), channel_id=1, source_target_pairs={{0,1},{1,2},{2,3},{3,4},{4,5},{5,6},{6,7},{7,8},{8,9},{9,10},{10,1... | collective-permute-start | bytes 3145736 | tf_op jit(solution)/shard_map/ppermute | solution.py:18
  353.7 21.3 %collective-permute-start.6 = (bf16[1024,128]{0,1:T(8,128)(2,1)}, bf16[1024,128]{0,1:T(8,128)(2,1)}, u32[]{:S(2)}, u32[]{:S(2)}) collective-permute-start(bf16[1024,128]{0,1:T(8,128)(2,1)} %collective-permute-done.4), channel_id=1, source_target_pairs={{0,1},{1,2},{2,3},{3,4},{4,5},{5,6},{6,7},{7,8},{8,9},{9,10},{10,1... | collective-permute-start | bytes 786440 | tf_op jit(solution)/shard_map/ppermute | solution.py:18
  389.7 24.7 %all-to-all-start.3 = ((bf16[2,512,512]{1,2,0:T(8,128)(2,1)}), bf16[2,512,512]{1,2,0:T(8,128)(2,1)S(1)}, u32[]{:S(2)}, u32[]{:S(2)}) async-start(bf16[2,512,512]{1,2,0:T(8,128)(2,1)} %copy.101), calls=%async_computation.3 | async-start | bytes 2097152 | tf_op jit(solution)/shard_map/all_to_all | solution.py:191
  393.5 460.2 %reduce-scatter.25.cloned.1.call-start = ((), (), s32[]{:S(2)}) async-start(), calls=%async_computation.30 | async-start | bytes 8454144 | tf_op jit(solution)/shard_map/reduce_scatter | solution.py:284
  519.5 339.6 %reduce-scatter.27.cloned.1.call-start = ((), (), s32[]{:S(2)}) async-start(), calls=%async_computation.31 | async-start | bytes 8454144 | tf_op jit(solution)/shard_map/reduce_scatter | solution.py:287
  527.3 337.0 %reduce-scatter.29.cloned.1.call-start = ((), (), s32[]{:S(2)}) async-start(), calls=%async_computation.32 | async-start | bytes 8454144 | tf_op jit(solution)/shard_map/reduce_scatter | solution.py:290
  552.1 26.5 %all-to-all-start.4 = ((bf16[512,2,512]{0,2,1:T(8,128)(2,1)}), bf16[512,2,512]{0,2,1:T(8,128)(2,1)S(1)}, u32[]{:S(2)}, u32[]{:S(2)}) async-start(bf16[512,2,512]{0,2,1:T(8,128)(2,1)} %bitcast.57), calls=%async_computation.4 | async-start | bytes 2097152 | tf_op jit(solution)/shard_map/all_to_all | solution.py:215
  594.3 55.9 %collective-permute-start.8 = (bf16[1024,8,16]{0,2,1:T(8,128)(2,1)}, bf16[1024,8,16]{0,2,1:T(8,128)(2,1)}, u32[]{:S(2)}, u32[]{:S(2)}) collective-permute-start(bf16[1024,8,16]{0,2,1:T(8,128)(2,1)} %convert_element_type.250), channel_id=1, source_target_pairs={{1,0},{2,1},{3,2},{4,3},{5,4},{6,5},{7,6},{8,7},{9,8},{10,9},{11,1... | collective-permute-start | bytes 786440 | tf_op jit(solution)/shard_map/ppermute | solution.py:18
  651.4 48.3 %collective-permute-start.9 = (bf16[1024,8,16]{0,2,1:T(8,128)(2,1)S(1)}, bf16[1024,8,16]{0,2,1:T(8,128)(2,1)S(1)}, u32[]{:S(2)}, u32[]{:S(2)}) collective-permute-start(bf16[1024,8,16]{0,2,1:T(8,128)(2,1)S(1)} %add_convert_fusion.7), channel_id=1, source_target_pairs={{1,0},{2,1},{3,2},{4,3},{5,4},{6,5},{7,6},{8,7},{9,8},{10,9},{11,1... | collective-permute-start | bytes 786440 | tf_op jit(solution)/shard_map/ppermute | solution.py:18
  655.4 46.8 %all-to-all-start.5 = ((bf16[2,512,128]{1,2,0:T(8,128)(2,1)}), bf16[2,512,128]{1,2,0:T(8,128)(2,1)S(1)}, u32[]{:S(2)}, u32[]{:S(2)}) async-start(bf16[2,512,128]{1,2,0:T(8,128)(2,1)} %copy.109), calls=%async_computation.5 | async-start | bytes 524288 | tf_op jit(solution)/shard_map/all_to_all | solution.py:260
  658.8 428.9 %reduce-scatter.17.cloned.1.call-start = ((), (), s32[]{:S(2)}) async-start(), calls=%async_computation.26 | async-start | bytes 1081344 | tf_op jit(solution)/shard_map/reduce_scatter | solution.py:277
  705.1 453.4 %reduce-scatter.19.cloned.1.call-start = ((), (), s32[]{:S(2)}) async-start(), calls=%async_computation.27 | async-start | bytes 1081344 | tf_op jit(solution)/shard_map/reduce_scatter | solution.py:278
  736.6 562.3 %reduce-scatter.23.cloned.1.call-start = ((), (), s32[]{:S(2)}) async-start(), calls=%async_computation.29 | async-start | bytes 4325376 | tf_op jit(solution)/shard_map/reduce_scatter | solution.py:280
  741.3 697.7 %reduce-scatter.21.cloned.1.call-start = ((), (), s32[]{:S(2)}) async-start(), calls=%async_computation.28 | async-start | bytes 4325376 | tf_op jit(solution)/shard_map/reduce_scatter | solution.py:279
  751.5 18.6 %collective-permute-start.13 = (bf16[1024,8,64]{0,2,1:T(8,128)(2,1)S(1)}, bf16[1024,8,64]{0,2,1:T(8,128)(2,1)S(1)}, u32[]{:S(2)}, u32[]{:S(2)}) collective-permute-start(bf16[1024,8,64]{0,2,1:T(8,128)(2,1)S(1)} %add_convert_fusion.2), channel_id=1, source_target_pairs={{1,0},{2,1},{3,2},{4,3},{5,4},{6,5},{7,6},{8,7},{9,8},{10,9},{11,1... | collective-permute-start | bytes 3145736 | tf_op jit(solution)/shard_map/ppermute | solution.py:18
  791.2 41.6 %collective-permute-start.15 = (bf16[1024,8,64]{0,2,1:T(8,128)(2,1)}, bf16[1024,8,64]{0,2,1:T(8,128)(2,1)}, u32[]{:S(2)}, u32[]{:S(2)}) collective-permute-start(bf16[1024,8,64]{0,2,1:T(8,128)(2,1)} %add_convert_fusion), channel_id=1, source_target_pairs={{1,0},{2,1},{3,2},{4,3},{5,4},{6,5},{7,6},{8,7},{9,8},{10,9},{11,1... | collective-permute-start | bytes 3145736 | tf_op jit(solution)/shard_map/ppermute | solution.py:18
  853.7 668.2 %reduce-scatter.31.cloned.1.call-start = ((), (), s32[]{:S(2)}) async-start(), calls=%async_computation.33 | async-start | bytes 6127616
  858.9 748.5 %reduce-scatter.33.cloned.1.call-start = ((), (), s32[]{:S(2)}) async-start(), calls=%async_computation.34 | async-start | bytes 6127616
  864.3 828.8 %reduce-scatter.35.cloned.1.call-start = ((), (), s32[]{:S(2)}) async-start(), calls=%async_computation.35 | async-start | bytes 6127616
  (70 other events, 2234.6 us)
Sparse Core Ops, SparseCore 0:
  10.3 47.0 all-gather.16
  59.7 42.6 all-gather.12
  105.3 54.8 all-gather.8
  162.3 46.9 all-gather.20
  211.9 59.6 all-gather.10
  273.0 74.7 all-gather.18
  349.4 80.9 all-gather.14
  431.9 69.4 all-gather.22
  519.6 112.1 reduce-scatter.24
  634.0 74.7 reduce-scatter.26
  711.1 71.3 reduce-scatter.28
  785.3 236.3 reduce-scatter.16
  1024.5 134.0 reduce-scatter.18
  1161.4 137.5 reduce-scatter.22
  1301.7 137.1 reduce-scatter.20
  1443.8 77.9 reduce-scatter.30
  1526.6 80.7 reduce-scatter.32
  1612.2 80.7 reduce-scatter.34
where the time goes:
time: 1710 us; the launch traced here: 1700 us
  waiting for transfers between devices  930 us (54%)
  blocking collectives  368 us (22%)
  matrix products  173 us (10%)
  local copies, waits for them, and re-layouts  77.7 us (5%)
  starting transfers between devices  69.1 us (4%)
  other arithmetic  33.1 us (2%)
  loops' own time  28.2 us (2%)
  between operations  21 us (1%)
    unnamed x21, waiting for transfers between devices  257 us
    unnamed x2, blocking collectives  241 us
    reduce_scatter x1, waiting for transfers between devices, body(): lax.psum_scatter(grad_wout, ('head', 'seq'), scatter_dimension=0, tiled=T...  140 us
    reduce_scatter x1, waiting for transfers between devices, body(): lax.psum_scatter(grad_wvalue, ('head', 'seq'), scatter_dimension=0, tiled...  140 us
    ppermute x16, waiting for transfers between devices, passed_along(): return lax.ppermute(block, axis, route)  115 us
    reduce_scatter x1, waiting for transfers between devices, body(): lax.psum_scatter(grad_wkey, ('head', 'seq'), scatter_dimension=0, tiled=T...  70.8 us
    all_gather x1, waiting for transfers between devices, body(): lax.all_gather(down_half, 'head', axis=0, tiled=True)  62.2 us
    ppermute x16, starting transfers between devices, passed_along(): return lax.ppermute(block, axis, route)  49.5 us
  transfers between devices with their start and end apart: 39, of which 20 were waited for; matrix products, arithmetic and copies ran while one was open for 15% of the time, Pallas kernels for 0%

commit v1 on v0

v1 whole, which is shorter than its diff:
```python
import functools

import jax
import jax.numpy as jnp
import numpy as np
from jax import lax
from jax.experimental import pallas as pl
from jax.experimental.pallas import tpu as pltpu
from jax.sharding import PartitionSpec as P

HEADS = 16
QD = 16
VD = 64
DOC_MAX = 4096
EPSILON = 1e-05
PAIRS = HEADS // 2
WIDE = 2 * VD
FEATS = 160
TILE = 256

BF = jnp.bfloat16
F32 = jnp.float32


def flip_seq(value, code):
    n = lax.axis_size("seq")
    return lax.ppermute(value, "seq", [(i, i ^ code) for i in range(n)])


def flip_head(value):
    n = lax.axis_size("head")
    return lax.ppermute(value, "head", [(i, i ^ 1) for i in range(n)])


def shift_seq(value, distance):
    n = lax.axis_size("seq")
    return lax.ppermute(
        value, "seq", [(i, i + distance) for i in range(n) if 0 <= i + distance < n]
    )


def layout():
    chips = lax.axis_size("seq") // 2
    near = 2 if chips <= 8 else 8
    far = chips // near
    return far, near


def place_kernel(groups, count, *refs):
    pieces, out, sem = refs[:count], refs[count], refs[count + 1]
    me = lax.axis_index("seq")
    head = lax.axis_index("head")
    n = lax.axis_size("seq")
    copies = []
    for piece, blocks in zip(pieces, groups):
        for index, (rel_head, rel_seq) in blocks:
            place = me ^ rel_seq
            if rel_head is not None:
                place = place + (head ^ rel_head) * n
            copies.append(
                pltpu.make_async_copy(piece.at[index], out.at[place], sem.at[len(copies)])
            )
    for copy in copies:
        copy.start()
    for copy in copies:
        copy.wait()


def place(pieces, groups, blocks):
    rows, cols = pieces[0].shape[-2:]
    total = sum(len(g) for g in groups)
    out = pl.pallas_call(
        functools.partial(place_kernel, groups, len(pieces)),
        out_shape=jax.ShapeDtypeStruct((blocks, rows, cols), pieces[0].dtype),
        in_specs=[pl.BlockSpec(memory_space=pl.ANY)] * len(pieces),
        out_specs=pl.BlockSpec(memory_space=pltpu.VMEM),
        scratch_shapes=[pltpu.SemaphoreType.DMA((total,))],
        compiler_params=pltpu.CompilerParams(vmem_limit_bytes=16 << 20),
        cost_estimate=pl.CostEstimate(
            flops=0, bytes_accessed=4 * blocks * rows * cols, transcendentals=0
        ),
        name="place",
    )(*pieces)
    return out.reshape(blocks * rows, cols)


def gather(shard, head_first):
    far, near = layout()
    far_codes = [2 * near * r for r in range(far)]
    near_codes = [2 * r for r in range(near)]
    if head_first:
        shard = jnp.stack([shard, flip_head(shard)])
    column = jnp.stack([shard] + [flip_seq(shard, code) for code in far_codes[1:]])
    held = [(column, 0, 0)]
    held += [(flip_seq(column, code), 0, code) for code in near_codes[1:]]
    if not head_first:
        held += [(flip_head(buf), 1, code) for buf, _, code in held]
    held += [(flip_seq(buf, 1), rel, code + 1) for buf, rel, code in held]
    result = []
    for buf, rel, code in held:
        if head_first:
            blocks = [((r, g), (g, code + far_codes[r])) for r in range(far) for g in range(2)]
        else:
            blocks = [((r,), (rel, code + far_codes[r])) for r in range(far)]
        result.append((buf, blocks))
    return result


def gather_rows(shard):
    got = gather(shard, False)
    return place([b for b, _ in got], [g for _, g in got], 2 * lax.axis_size("seq"))


def gather_halves(shard, head_first):
    got = gather(shard, head_first)
    halves = []
    for rel in range(2):
        pieces, groups = [], []
        for buf, blocks in got:
            mine = [(i, (None, code)) for i, (r, code) in blocks if r == rel]
            if mine:
                pieces.append(buf)
                groups.append(mine)
        halves.append(place(pieces, groups, lax.axis_size("seq")))
    return halves


def add_low(*terms):
    total = terms[0].astype(F32)
    for term in terms[1:]:
        total = total + term.astype(F32)
    return total.astype(BF)


def pick(value, index, axis):
    return lax.dynamic_index_in_dim(value, index, axis, keepdims=False)


def scatter(grads, head_first):
    far, near = layout()
    seq = lax.axis_index("seq")
    far_at, near_at = seq // (2 * near), (seq // 2) % near
    both = [
        add_low(grads[rel][0], flip_seq(grads[rel][1], 1)) for rel in range(2)
    ]
    rows = both[0].shape[0] // (far * near)
    cols = both[0].shape[1]
    if head_first:
        whole = add_low(both[0], flip_head(both[1])).reshape(far, near, rows, cols)
    else:
        whole = jnp.stack(both).reshape(2, far, near, rows, cols).transpose(1, 2, 0, 3, 4)
    parts = [pick(whole, near_at, 1)]
    parts += [flip_seq(pick(whole, near_at ^ r, 1), 2 * r) for r in range(1, near)]
    column = add_low(*parts)
    parts = [pick(column, far_at, 0)]
    parts += [flip_seq(pick(column, far_at ^ r, 0), 2 * near * r) for r in range(1, far)]
    if head_first:
        return sum(part.astype(F32) for part in parts)
    both = add_low(*parts)
    return both[0].astype(F32) + flip_head(both[1]).astype(F32)


def sum_everywhere(value):
    value = value + flip_head(value)
    code = 1
    while code < lax.axis_size("seq"):
        value = value + flip_seq(value, code)
        code *= 2
    return value


def feature_table():
    first, second, one, two, scale = [], [], [], [], []
    for a in range(QD):
        for b in range(a, QD):
            first.append(a)
            second.append(b)
            one.append(0.0)
            two.append(0.0)
            scale.append((1.0 if a == b else 2.0) / (2.0 * QD))
    for a in range(QD):
        first.append(a)
        second.append(-1000)
        one.append(0.0)
        two.append(1.0)
        scale.append(QD**-0.5)
    first.append(-1000)
    second.append(-1000)
    one.append(1.0)
    two.append(1.0)
    scale.append(1.0)
    pad = FEATS - len(first)
    table = np.zeros((8, FEATS), np.float32)
    table[0] = np.array(first + [-1000] * pad)
    table[1] = np.array(second + [-1000] * pad)
    table[2] = np.array(one + [0.0] * pad)
    table[3] = np.array(two + [0.0] * pad)
    table[4] = np.array(scale + [0.0] * pad)
    return table


def mm(a, b, dims):
    return lax.dot_general(a, b, ((dims[0], dims[1]), ((), ())), preferred_element_type=F32)


NN = ((1,), (0,))
NT = ((1,), (1,))
TN = ((0,), (0,))


def selectors(table, head):
    lanes = HEADS * QD
    row = (lax.broadcasted_iota(jnp.int32, (lanes, FEATS), 0) - head * QD).astype(F32)
    one = (row == table[0:1, :]).astype(F32).astype(BF)
    two = (row == table[1:2, :]).astype(F32).astype(BF)
    return one, two


def factors(values, table, sel):
    return (
        mm(values, sel[0], NN) + table[2:3, :],
        mm(values, sel[1], NN) + table[3:4, :],
    )


def half_mask(rows, part):
    lane = lax.broadcasted_iota(jnp.int32, (rows, WIDE), 1)
    return (lane >= VD) if part else (lane < VD)


def head_mask(rows, head):
    lane = lax.broadcasted_iota(jnp.int32, (rows, HEADS * QD), 1)
    return (lane >= head * QD) & (lane < (head + 1) * QD)


def keep(mask, value):
    return jnp.where(mask, value.astype(F32), 0.0).astype(BF)


def state_kernel(table_ref, keys_ref, values_ref, last_ref, wide_ref, thin_ref):
    pair = pl.program_id(0)
    table = table_ref[...]
    keys = keys_ref[...]
    rows = keys.shape[0]
    last = last_ref[...]
    total = None
    for part in range(2):
        sel = selectors(table, 2 * pair + part)
        one, two = factors(keys, table, sel)
        phi = one * two * last
        value = keep(half_mask(rows, part), values_ref[...])
        new = mm(phi.astype(BF), value, TN)
        total = new if total is None else total + new
        thin_ref[0, part : part + 1, :] = jnp.sum(phi, axis=0, keepdims=True)
    thin_ref[0, 2:, :] = jnp.zeros((6, FEATS), F32)
    wide_ref[0] = total.astype(BF)


def visible_tile(mask_ref, row_ids_ref, col_ids_ref, rows):
    for i in range(rows // TILE):
        for j in range(i + 1):
            same = (
                row_ids_ref[i * TILE : (i + 1) * TILE, :]
                == col_ids_ref[:, j * TILE : (j + 1) * TILE]
            )
            if i == j:
                same = same & (
                    lax.broadcasted_iota(jnp.int32, (TILE, TILE), 1)
                    <= lax.broadcasted_iota(jnp.int32, (TILE, TILE), 0)
                )
            mask_ref[i * TILE : (i + 1) * TILE, j * TILE : (j + 1) * TILE] = same.astype(F32)


def local_kernel(
    query_ref, keys_ref, values_ref, row_ids_ref, col_ids_ref, num_ref, den_ref, mask_ref
):
    pair = pl.program_id(0)
    rows = query_ref.shape[0]

    @pl.when(pair == 0)
    def _():
        visible_tile(mask_ref, row_ids_ref, col_ids_ref, rows)

    for i in range(rows // TILE):
        here = slice(i * TILE, (i + 1) * TILE)
        num = jnp.zeros((TILE, WIDE), F32)
        dens = []
        for part in range(2):
            head = 2 * pair + part
            query = keep(head_mask(TILE, head), query_ref[here, :] * (QD**-0.5))
            den = jnp.zeros((TILE, 1), F32)
            for j in range(i + 1):
                there = slice(j * TILE, (j + 1) * TILE)
                s = mm(query, keys_ref[there, :], NT)
                w = (1.0 + s + 0.5 * s * s) * mask_ref[here, there]
                den = den + jnp.sum(w, axis=1, keepdims=True)
                num = num + mm(
                    w.astype(BF), keep(half_mask(TILE, part), values_ref[there, :]), NN
                )
            dens.append(den)
        num_ref[here, :] = num
        den_ref[here, :] = jnp.where(half_mask(TILE, 0), dens[0], dens[1])


def finish_kernel(
    table_ref, query_ref, num_ref, den_ref, first_ref, wide_ref, thin_ref, out_ref, rden_ref
):
    pair = pl.program_id(0)
    table = table_ref[...]
    query = query_ref[...]
    rows = query.shape[0]
    first = first_ref[...]
    num, den = num_ref[...], den_ref[...]
    for part in range(2):
        sel = selectors(table, 2 * pair + part)
        one, two = factors(query, table, sel)
        phi = one * two * (table[4:5, :] * first)
        mask = half_mask(rows, part)
        extra = mm(phi.astype(BF), wide_ref[0], NN)
        num = num + jnp.where(mask, extra, 0.0)
        more = jnp.sum(phi * thin_ref[0, part : part + 1, :], axis=1, keepdims=True)
        den = den + jnp.where(mask, more, 0.0)
    rden = 1.0 / den
    rden_ref[...] = rden
    out_ref[...] = (num * rden).astype(BF)


def prepare(grad_ref, out_ref, rden_ref):
    rows = grad_ref.shape[0]
    grad = grad_ref[...].astype(F32)
    rden = rden_ref[...]
    dnum = (grad * rden).astype(BF)
    prod = grad * out_ref[...].astype(F32) * rden
    deltas = [
        jnp.sum(jnp.where(half_mask(rows, part), prod, 0.0), axis=1, keepdims=True)
        for part in range(2)
    ]
    return dnum, deltas


def grad_state_kernel(
    table_ref, query_ref, grad_ref, out_ref, rden_ref, first_ref, wide_ref, thin_ref
):
    pair = pl.program_id(0)
    table = table_ref[...]
    query = query_ref[...]
    rows = query.shape[0]
    dnum, deltas = prepare(grad_ref, out_ref, rden_ref)
    total = None
    for part in range(2):
        sel = selectors(table, 2 * pair + part)
        one, two = factors(query, table, sel)
        phi = one * two * (table[4:5, :] * first_ref[...])
        new = mm(phi.astype(BF), keep(half_mask(rows, part), dnum), TN)
        total = new if total is None else total + new
        thin_ref[0, part : part + 1, :] = -jnp.sum(phi * deltas[part], axis=0, keepdims=True)
    thin_ref[0, 2:, :] = jnp.zeros((6, FEATS), F32)
    wide_ref[0] = total.astype(BF)


def local_grad_kernel(
    table_ref,
    query_ref,
    keys_ref,
    values_ref,
    grad_ref,
    out_ref,
    rden_ref,
    row_ids_ref,
    col_ids_ref,
    first_ref,
    wide_ref,
    thin_ref,
    dq_ref,
    dk_ref,
    dv_ref,
    mask_ref,
    dq_acc,
    dk_acc,
):
    pair = pl.program_id(0)
    table = table_ref[...]
    query = query_ref[...]
    keys = keys_ref[...]
    rows = query.shape[0]
    tiles = rows // TILE
    scale = QD**-0.5

    @pl.when(pair == 0)
    def _():
        visible_tile(mask_ref, row_ids_ref, col_ids_ref, rows)
        dq_acc[...] = jnp.zeros_like(dq_acc)
        dk_acc[...] = jnp.zeros_like(dk_acc)

    dnum, deltas = prepare(grad_ref, out_ref, rden_ref)
    dv = [jnp.zeros((TILE, WIDE), F32) for _ in range(tiles)]
    for part in range(2):
        head = 2 * pair + part
        at_head = head_mask(rows, head)
        q_head = keep(at_head, query * scale)
        k_head = keep(at_head, keys * scale)
        d_head = keep(half_mask(rows, part), dnum)
        for i in range(tiles):
            here = slice(i * TILE, (i + 1) * TILE)
            dq = dq_acc[here, :]
            for j in range(i + 1):
                there = slice(j * TILE, (j + 1) * TILE)
                s = mm(q_head[here], keys[there], NT)
                mask = mask_ref[here, there]
                w = ((1.0 + s + 0.5 * s * s) * mask).astype(BF)
                dp = mm(d_head[here], values_ref[there, :], NT)
                ds = ((dp - deltas[part][here]) * ((1.0 + s) * mask)).astype(BF)
                dq = dq + mm(ds, k_head[there], NN)
                dk_acc[there, :] += mm(ds, q_head[here], TN)
                dv[j] = dv[j] + mm(w, d_head[here], TN)
            dq_acc[here, :] = dq
        sel = selectors(table, head)
        one, two = factors(query, table, sel)
        dphi = mm(d_head, wide_ref[0], NT) - deltas[part] * thin_ref[0, part : part + 1, :]
        dphi = dphi * (table[4:5, :] * first_ref[...])
        dq_acc[...] += mm((dphi * two).astype(BF), sel[0], NT) + mm(
            (dphi * one).astype(BF), sel[1], NT
        )
    for j in range(tiles):
        dv_ref[j * TILE : (j + 1) * TILE, :] = dv[j]

    @pl.when(pair == PAIRS - 1)
    def _():
        dq_ref[...] = dq_acc[...].astype(BF)
        dk_ref[...] = dk_acc[...]


def finish_grad_kernel(
    table_ref, keys_ref, values_ref, dk_in_ref, dv_in_ref, last_ref, wide_ref, thin_ref,
    dk_ref, dv_ref, dk_acc,
):
    pair = pl.program_id(0)
    table = table_ref[...]
    keys = keys_ref[...]
    rows = keys.shape[0]
    last = last_ref[...]

    @pl.when(pair == 0)
    def _():
        dk_acc[...] = dk_in_ref[...]

    dv = dv_in_ref[...]
    for part in range(2):
        sel = selectors(table, 2 * pair + part)
        one, two = factors(keys, table, sel)
        mask = half_mask(rows, part)
        phi = one * two * last
        dv = dv + jnp.where(mask, mm(phi.astype(BF), wide_ref[0], NN), 0.0)
        dphi = mm(keep(mask, values_ref[...]), wide_ref[0], NT) + thin_ref[0, part : part + 1, :]
        dphi = dphi * last
        dk_acc[...] += mm((dphi * two).astype(BF), sel[0], NT) + mm(
            (dphi * one).astype(BF), sel[1], NT
        )
    dv_ref[...] = dv.astype(BF)

    @pl.when(pair == PAIRS - 1)
    def _():
        dk_ref[...] = dk_acc[...].astype(BF)


def full_spec(shape):
    return pl.BlockSpec(shape, lambda p: (0,) * len(shape))


def pair_spec(rows):
    return pl.BlockSpec((rows, WIDE), lambda p: (0, p))


def state_specs():
    return [
        pl.BlockSpec((1, FEATS, WIDE), lambda p: (p, 0, 0)),
        pl.BlockSpec((1, 8, FEATS), lambda p: (p, 0, 0)),
    ]


STATE_SHAPES = (
    jax.ShapeDtypeStruct((PAIRS, FEATS, WIDE), BF),
    jax.ShapeDtypeStruct((PAIRS, 8, FEATS), F32),
)


def run(kernel, in_specs, out_specs, out_shape, args, scratch=(), flops=0):
    moved = sum(a.size * a.dtype.itemsize for a in args)
    return pl.pallas_call(
        kernel,
        grid=(PAIRS,),
        in_specs=in_specs,
        out_specs=out_specs,
        out_shape=out_shape,
        scratch_shapes=scratch,
        compiler_params=pltpu.CompilerParams(vmem_limit_bytes=48 << 20),
        cost_estimate=pl.CostEstimate(flops=flops, bytes_accessed=moved, transcendentals=0),
        name=kernel.__name__,
    )(*args)


def exchange(wide, thin, ids, rows, forward):
    head, seq = lax.axis_index("head"), lax.axis_index("seq")
    n = lax.axis_size("seq")
    segments = 2 * n
    firsts = ids.reshape(segments, rows)[:, 0]
    lasts = ids.reshape(segments, rows)[:, rows - 1]
    step = 1 if forward else -1
    near_end, far_end = (lasts, firsts) if forward else (firsts, lasts)

    def end_of(which, segment):
        return which[jnp.clip(segment, 0, segments - 1)]

    seg = 2 * seq + head
    takes = end_of(far_end, seg)
    core = seq % 2
    late_head = head if forward else 1 - head
    late_core = core if forward else 1 - core

    def gate(flag):
        return jnp.where(flag, 1.0, 0.0).astype(F32)

    def wider(state):
        return [part.astype(F32) for part in state]

    def narrow(state):
        return [state[0].astype(BF), state[1]]

    def merge(own, other, late, other_takes, joined):
        gained = [part * (gate(other_takes) * late) for part in other]
        own_factor = jnp.where(late == 1, 1.0, gate(joined))
        other_factor = jnp.where(late == 1, gate(joined), 1.0)
        joint = [a * own_factor + b * other_factor for a, b in zip(own, other)]
        return gained, joint

    own = [wide, thin]
    other = [flip_head(part) for part in own]
    first_of, second_of = 2 * seq, 2 * seq + 1
    if not forward:
        first_of, second_of = second_of, first_of
    total, joint = merge(
        wider(own),
        wider(other),
        late_head,
        end_of(near_end, seg - step) == takes,
        end_of(near_end, first_of) == end_of(near_end, second_of),
    )
    joint = narrow(joint)
    other = [flip_seq(part, 1) for part in joint]
    base = 4 * (seq // 2)
    early_end, late_end = (base + 1, base + 3) if forward else (base + 2, base)
    gained, joint = merge(
        wider(joint),
        wider(other),
        late_core,
        end_of(near_end, early_end) == takes,
        end_of(near_end, early_end) == end_of(near_end, late_end),
    )
    total = [a + b for a, b in zip(total, gained)]
    joint = narrow(joint)
    half = PAIRS // 2
    mine = [lax.dynamic_slice_in_dim(part, core * half, half, 0) for part in joint]
    hops = -(-DOC_MAX // (4 * rows))
    far = None
    for hop in range(1, hops + 1):
        got = wider([shift_seq(part, 2 * hop * step) for part in mine])
        nearer, farther = late_end - 4 * step, late_end - 4 * step * hop
        joined = gate(end_of(near_end, nearer) == end_of(near_end, farther))
        got = [part * joined for part in got]
        far = got if far is None else [a + b for a, b in zip(far, got)]
    far = narrow(far)
    other = [flip_seq(part, 1) for part in far]
    comes = (seq // 2 >= 1) if forward else (seq // 2 < n // 2 - 1)
    use = gate(comes & (end_of(near_end, late_end - 4 * step) == takes))
    result = []
    for a, b, so_far in zip(far, other, total):
        low = jnp.where(core == 0, a, b).astype(F32)
        high = jnp.where(core == 0, b, a).astype(F32)
        result.append(so_far + use * jnp.concatenate([low, high], axis=0))
    return narrow(result)


def rms_scale(values, gain):
    return values * lax.rsqrt(jnp.mean(values * values, axis=-1, keepdims=True) + EPSILON) * gain


def swish_mix(gate, up_proj):
    return jax.nn.silu(gate) * up_proj


def dot_nn(a, b):
    return jnp.dot(a, b, preferred_element_type=F32)


def dot_nt(a, b):
    return lax.dot_general(a, b, (((1,), (1,)), ((), ())), preferred_element_type=F32)


def dot_tn(a, b):
    return lax.dot_general(a, b, (((0,), (0,)), ((), ())), preferred_element_type=F32)


def row_grads(left, right, by_head):
    head, core = lax.axis_index("head"), lax.axis_index("seq") % 2
    tokens = left.shape[0]
    chips = lax.axis_size("seq") // 2
    heads = 2 if by_head else 1
    rows = left.shape[1] // (heads * chips * 2)
    split = left.reshape(tokens, heads, chips, 2, rows)
    out = []
    for rel in range(heads):
        plane = pick(split, head ^ rel, 1) if by_head else split[:, 0]
        out.append([pick(plane, core ^ r, 2).reshape(tokens, chips * rows) for r in range(2)])
    if by_head:
        return [[dot_tn(part, right).astype(BF) for part in parts] for parts in out]
    return [[dot_tn(part, r).astype(BF) for part in out[0]] for r in right]


def body(
    layer_input,
    segment_ids,
    norm1_gain,
    w_query,
    w_key,
    w_value,
    w_out,
    norm2_gain,
    w_gate,
    w_up,
    w_down,
    output_grad,
):
    rows = layer_input.shape[1]
    head, seq = lax.axis_index("head"), lax.axis_index("seq")
    n_seq = lax.axis_size("seq")
    qk = HEADS * QD
    inputs = layer_input[0].astype(F32)
    width = inputs.shape[1]

    slot = head * n_seq + seq
    small = norm1_gain.shape[0]
    gains = jnp.zeros((2, width // small, small), F32)
    gains = lax.dynamic_update_slice(
        gains, jnp.stack([norm1_gain, norm2_gain]).astype(F32)[:, None, :], (0, slot, 0)
    ).reshape(2, width)
    gains = sum_everywhere(gains)
    gain_first, gain_second = gains[0], gains[1]

    qkv_full = gather_rows(jnp.concatenate([w_query, w_key, w_value], axis=1))
    out_full = gather_rows(w_out)
    gate_w = gather_halves(w_gate, False)
    up_w = gather_halves(w_up, False)
    down_w = gather_halves(w_down.T, True)

    segment = 2 * seq + head
    ids = lax.dynamic_slice_in_dim(segment_ids, segment * rows, rows)
    row_ids, col_ids = ids[:, None], ids[None, :]
    first = (row_ids == ids[0]).astype(F32)
    last = (row_ids == ids[rows - 1]).astype(F32)
    table = jnp.asarray(feature_table())

    normed_one = rms_scale(inputs, gain_first).astype(BF)
    qkv = dot_nn(normed_one, qkv_full).astype(BF)
    query, keys, values = qkv[:, :qk], qkv[:, qk : 2 * qk], qkv[:, 2 * qk :]
    vcols = HEADS * VD
    t_spec, q_spec = full_spec((8, FEATS)), full_spec((rows, qk))
    one_spec, row_spec = full_spec((rows, 1)), full_spec((1, rows))
    p_spec = pair_spec(rows)
    f32_like = jax.ShapeDtypeStruct((rows, vcols), F32)
    bf_like = jax.ShapeDtypeStruct((rows, vcols), BF)
    state = run(
        state_kernel,
        [t_spec, q_spec, p_spec, one_spec],
        state_specs(),
        STATE_SHAPES,
        (table, keys, values, last),
        flops=8 * rows * qk * FEATS * HEADS,
    )
    num, den = run(
        local_kernel,
        [q_spec, q_spec, p_spec, one_spec, row_spec],
        [p_spec, p_spec],
        [f32_like, f32_like],
        (query, keys, values, row_ids, col_ids),
        [pltpu.VMEM((rows, rows), F32)],
        flops=8 * rows * rows * qk * HEADS,
    )
    before = exchange(*state, segment_ids, rows, True)
    attended, rden = run(
        finish_kernel,
        [t_spec, q_spec, p_spec, p_spec, one_spec] + state_specs(),
        [p_spec, p_spec],
        [bf_like, f32_like],
        (table, query, num, den, first, *before),
        flops=8 * rows * qk * FEATS * HEADS,
    )
    residual = inputs + dot_nn(attended, out_full)
    normed_two = rms_scale(residual, gain_second).astype(BF)

    grad_output = output_grad[0]
    outcome = residual
    grad_normed_two = None
    hiddens, grad_gates, grad_ups = [], [], []
    for w_g, w_u, w_d in zip(gate_w, up_w, down_w):
        gate = dot_nn(normed_two, w_g)
        up_proj = dot_nn(normed_two, w_u)
        grad_hidden = dot_nn(grad_output, w_d)
        hidden, mix_pull = jax.vjp(swish_mix, gate, up_proj)
        grad_gate, grad_up = mix_pull(grad_hidden)
        hiddens.append(hidden.astype(BF))
        grad_gates.append(grad_gate.astype(BF))
        grad_ups.append(grad_up.astype(BF))
        outcome = outcome + dot_nt(hiddens[-1], w_d)
        more = dot_nt(grad_gates[-1], w_g) + dot_nt(grad_ups[-1], w_u)
        grad_normed_two = more if grad_normed_two is None else grad_normed_two + more
    outcome = outcome.astype(BF)
    d_gate = scatter(row_grads(normed_two, grad_gates, False), True)
    d_up = scatter(row_grads(normed_two, grad_ups, False), True)
    d_down = scatter(row_grads(grad_output, hiddens, False), False).T

    _, norm_pull = jax.vjp(rms_scale, residual, gain_second)
    grad_resid_two, grad_gain_two = norm_pull(grad_normed_two)
    grad_middle = grad_output.astype(F32) + grad_resid_two
    grad_middle_low = grad_middle.astype(BF)
    d_out = scatter(row_grads(attended, grad_middle_low, True), True)
    grad_attended = dot_nt(grad_middle_low, out_full).astype(BF)

    grad_state = run(
        grad_state_kernel,
        [t_spec, q_spec, p_spec, p_spec, p_spec, one_spec],
        state_specs(),
        STATE_SHAPES,
        (table, query, grad_attended, attended, rden, first),
        flops=8 * rows * qk * FEATS * HEADS,
    )
    qk_f32 = jax.ShapeDtypeStruct((rows, qk), F32)
    qk_bf = jax.ShapeDtypeStruct((rows, qk), BF)
    grad_query, grad_key, grad_value = run(
        local_grad_kernel,
        [t_spec, q_spec, q_spec, p_spec, p_spec, p_spec, p_spec, one_spec, row_spec, one_spec]
        + state_specs(),
        [q_spec, q_spec, p_spec],
        [qk_bf, qk_f32, f32_like],
        (table, query, keys, values, grad_attended, attended, rden, row_ids, col_ids, first)
        + tuple(before),
        [pltpu.VMEM((rows, rows), F32), pltpu.VMEM((rows, qk), F32), pltpu.VMEM((rows, qk), F32)],
        flops=20 * rows * rows * qk * HEADS,
    )
    after = exchange(*grad_state, segment_ids, rows, False)
    grad_key, grad_value = run(
        finish_grad_kernel,
        [t_spec, q_spec, p_spec, q_spec, p_spec, one_spec] + state_specs(),
        [q_spec, p_spec],
        [qk_bf, bf_like],
        (table, keys, values, grad_key, grad_value, last, *after),
        [pltpu.VMEM((rows, qk), F32)],
        flops=16 * rows * qk * FEATS * HEADS,
    )
    grad_qkv = jnp.concatenate([grad_query, grad_key, grad_value], axis=1)
    d_qkv = scatter(row_grads(normed_one, grad_qkv, True), True)
    grad_normed_one = dot_nt(grad_qkv, qkv_full)
    _, first_pull = jax.vjp(rms_scale, inputs, gain_first)
    grad_inputs, grad_gain_one = first_pull(grad_normed_one)
    grad_layer = grad_middle + grad_inputs
    grad_gains = sum_everywhere(jnp.stack([grad_gain_one, grad_gain_two]))
    grad_gains = lax.dynamic_slice_in_dim(
        grad_gains.reshape(2, width // small, small), slot, 1, 1
    )[:, 0]
    return (
        outcome[None],
        grad_layer[None],
        grad_gains[0],
        d_qkv[:, :qk],
        d_qkv[:, qk : 2 * qk],
        d_qkv[:, 2 * qk :],
        d_out,
        grad_gains[1],
        d_gate,
        d_up,
        d_down,
    )


def solution(mesh):
    split = P(("head", "seq"))
    rows = P(("head", "seq"), None)
    block = P("seq", "head", None)
    wide, tall = P("seq", "head"), P("head", "seq")
    in_specs = (block, P(), split, rows, rows, rows, rows, split, wide, wide, tall, block)
    out_specs = (block, block, split, rows, rows, rows, rows, split, wide, wide, tall)
    return jax.shard_map(body, mesh=mesh, in_specs=in_specs, out_specs=out_specs, check_vma=False)
```

time: 1710 us -> 641 us (0.37)
  waiting for transfers between devices: 930 us -> 224 us
  blocking collectives: 368 us -> 0 us
  Pallas kernels: 0 us -> 96.8 us
  matrix products: 173 us -> 87.6 us
  starting transfers between devices: 69.1 us -> 116 us
  loops' own time: 28.2 us -> 0 us
  local copies, waits for them, and re-layouts: 77.7 us -> 51.9 us
    reduce_scatter x7 -> x0, waiting for transfers between devices: 351 us -> none  [the longest x1 140 us: body(): lax.psum_scatter(grad_wout, ('head', 'seq'), scatter_dimension=0, tiled=T...]
    unnamed x21 -> x0, waiting for transfers between devices: 257 us -> none
    unnamed x2 -> x0, blocking collectives: 241 us -> none
    all_gather x8 -> x0, waiting for transfers between devices: 164 us -> none  [the longest x1 62.2 us: body(): lax.all_gather(down_half, 'head', axis=0, tiled=True)]
    ppermute x16 -> x112, waiting for transfers between devices: 115 us -> 224 us  [the longest x84 122 us: flip_seq(): return lax.ppermute(value, 'seq', [(i, i ^ code) for i in range(n)])]
    pallas_call x0 -> x14, Pallas kernels: none -> 96.8 us  [the longest x6 71.1 us: run(): pl.pallas_call(kernel, grid=(PAIRS,), in_specs=in_specs, out_specs=out_sp...]
    all_gather x2 -> x0, blocking collectives: 87.8 us -> none  [the longest x1 46.8 us: body(): lax.all_gather(w_key, ('head', 'seq'), axis=0, tiled=True)]
    dot_general x27 -> x36, matrix products: 173 us -> 87.6 us  [the longest x20 41.1 us: dot_tn(): lax.dot_general(a, b, (((0,), (0,)), ((), ())), preferred_element_type=F32)]
  transfers between devices with their start and end apart: 39 -> 112, of which waited for: 20 -> 37; matrix products, arithmetic and copies ran while one was open for 15% -> 17% of each run, Pallas kernels for 0% -> 8%
where the time goes in v1:
time: 641 us; the launch traced here: 632 us
  waiting for transfers between devices  224 us (35%)
  starting transfers between devices  116 us (18%)
  Pallas kernels  96.8 us (15%)
  matrix products  87.6 us (14%)
  local copies, waits for them, and re-layouts  51.9 us (8%)
  other arithmetic  38.4 us (6%)
  between operations  18 us (3%)
    ppermute x84, waiting for transfers between devices, flip_seq(): return lax.ppermute(value, 'seq', [(i, i ^ code) for i in range(n)])  122 us
    ppermute x20, waiting for transfers between devices, flip_head(): return lax.ppermute(value, 'head', [(i, i ^ 1) for i in range(n)])  81 us
    pallas_call x6, Pallas kernels, run(): pl.pallas_call(kernel, grid=(PAIRS,), in_specs=in_specs, out_specs=out_sp...  71.1 us
    ppermute x84, starting transfers between devices, flip_seq(): return lax.ppermute(value, 'seq', [(i, i ^ code) for i in range(n)])  68.9 us
    dot_general x20, matrix products, dot_tn(): lax.dot_general(a, b, (((0,), (0,)), ((), ())), preferred_element_type=F32)  41.1 us
    dot_general x8, matrix products, dot_nn(): return jnp.dot(a, b, preferred_element_type=F32)  27.3 us
    pallas_call x8, Pallas kernels, place(): pl.pallas_call(functools.partial(place_kernel, groups, len(pieces)), out_...  25.7 us
    ppermute x8, starting transfers between devices, shift_seq(): lax.ppermute(value, 'seq', [(i, i + distance) for i in range(n) if 0 <= i...  24.8 us
  transfers between devices with their start and end apart: 112, of which 37 were waited for; matrix products, arithmetic and copies ran while one was open for 17% of the time, Pallas kernels for 8%

profile of v1, /device:TPU:0, one launch (start us, length us, event | category | flops | bytes accessed | tf_op | source)
XLA Modules:
  0.0 632.3 jit_solution(9836527692617555239)
XLA Ops:
  3.0 5.0 collective-permute-start.7
  15.8 4.3 collective-permute-done.6
  62.5 4.3 collective-permute-done.43
  66.9 7.2 %collective-permute-done.42 = bf16[64,1376]{1,0:T(8,128)(2,1)} collective-permute-done((bf16[64,1376]{1,0:T(8,128)(2,1)S(1)}, bf16[64,1376]{1,0:T(8,128)(2,1)}, u32[]{:S(2)}, u32[]{:S(2)}) %collective-permute-start.42) | collective-permute-done | bytes 176160 | tf_op jit(solution)/shard_map/ppermute | solution.py:27
  82.9 5.1 place.8
  90.6 6.1 state_kernel.1
  99.4 9.3 %collective-permute-done.20 = f32[8,8,160]{2,1,0:T(8,128)S(1)} collective-permute-done((f32[8,8,160]{2,1,0:T(8,128)S(1)}, f32[8,8,160]{2,1,0:T(8,128)S(1)}, u32[]{:S(2)}, u32[]{:S(2)}) %collective-permute-start.20) | collective-permute-done | bytes 40992 | tf_op jit(solution)/shard_map/ppermute | solution.py:32
  112.4 4.9 collective-permute-done.35
  123.2 7.2 %collective-permute-done.50 = bf16[2,64,1376]{2,1,0:T(8,128)(2,1)S(1)} collective-permute-done((bf16[2,64,1376]{2,1,0:T(8,128)(2,1)S(1)}, bf16[2,64,1376]{2,1,0:T(8,128)(2,1)S(1)}, u32[]{:S(2)}, u32[]{:S(2)}) %collective-permute-start.50) | collective-permute-done | bytes 352288 | tf_op jit(solution)/shard_map/ppermute | solution.py:27
  131.1 20.5 %collective-permute-done.49 = bf16[2,64,1376]{2,1,0:T(8,128)(2,1)S(1)} collective-permute-done((bf16[2,64,1376]{2,1,0:T(8,128)(2,1)S(1)}, bf16[2,64,1376]{2,1,0:T(8,128)(2,1)S(1)}, u32[]{:S(2)}, u32[]{:S(2)}) %collective-permute-start.49) | collective-permute-done | bytes 352288 | tf_op jit(solution)/shard_map/ppermute | solution.py:27
  157.9 10.1 %collective-permute-done.22 = f32[4,8,160]{2,1,0:T(8,128)S(1)} collective-permute-done((f32[4,8,160]{2,1,0:T(8,128)S(1)}, f32[4,8,160]{2,1,0:T(8,128)S(1)}, u32[]{:S(2)}, u32[]{:S(2)}) %collective-permute-start.22) | collective-permute-done | bytes 20512 | tf_op jit(solution)/shard_map/ppermute | solution.py:37
  169.8 10.0 %collective-permute-start.18 = (bf16[4,160,128]{2,1,0:T(8,128)(2,1)S(1)}, bf16[4,160,128]{2,1,0:T(8,128)(2,1)S(1)}, u32[]{:S(2)}, u32[]{:S(2)}) collective-permute-start(bf16[4,160,128]{2,1,0:T(8,128)(2,1)S(1)} %fusion.64), channel_id=1, source_target_pairs={{0,4},{1,5},{2,6},{3,7},{4,8},{5,9},{6,10},{7,11},{8,12},{9,13},{1... | collective-permute-start | bytes 491528 | tf_op jit(solution)/shard_map/ppermute | solution.py:37
  179.8 4.7 collective-permute-start.17
  190.0 8.3 %local_kernel.1 = (f32[512,1024]{1,0:T(8,128)S(1)}, f32[512,1024]{1,0:T(8,128)S(1)}) custom-call(bf16[512,256]{1,0:T(8,128)(2,1)S(1)} %get-tuple-element.50.query_ref, bf16[512,256]{1,0:T(8,128)(2,1)S(1)} %get-tuple-element.49.keys_ref, bf16[512,1024]{1,0:T(8,128)(2,1)S(1)} %slice.71.values_ref, s32[512,1]{1,0:T(8,128)S(1)} %copy.32.row_ids_ref, ...), custom_call_target="tpu_custom_call" | custom-call | flops 8589934592 | bytes 1576960 | tf_op jit(solution)/shard_map/local_kernel/pallas_call | solution.py:489
  214.9 8.0 %finish_kernel.1 = (bf16[512,1024]{1,0:T(8,128)(2,1)S(1)}, f32[512,1024]{1,0:T(8,128)S(1)}) custom-call(f32[8,160]{1,0:T(8,128)S(1)} %copy-done.20, bf16[512,256]{1,0:T(8,128)(2,1)S(1)} %get-tuple-element.50.query_ref, f32[512,1024]{1,0:T(8,128)S(1)} %copy-done.24, f32[512,1024]{1,0:T(8,128)} %copy-done.25, f32[512,1]{1,0:T(8,128)S(1)} %copy-done.12, ...), custom_call_target="tpu_custom_call" | custom-call | flops 2684354560 | bytes 4832256 | tf_op jit(solution)/shard_map/finish_kernel/pallas_call | solution.py:489
  244.7 7.8 %collective-permute-done.55.refs_1_ = bf16[4,64,1376]{2,1,0:T(8,128)(2,1)} collective-permute-done((bf16[4,64,1376]{2,1,0:T(8,128)(2,1)}, bf16[4,64,1376]{2,1,0:T(8,128)(2,1)}, u32[]{:S(2)}, u32[]{:S(2)}) %collective-permute-start.55) | collective-permute-done | bytes 704544 | tf_op jit(solution)/shard_map/ppermute | solution.py:32
  264.2 4.4 place.15
  271.9 6.1 fusion.12
  301.2 29.4 %local_grad_kernel.1 = (bf16[512,256]{1,0:T(8,128)(2,1)S(1)}, f32[512,256]{1,0:T(8,128)S(1)}, f32[512,1024]{1,0:T(8,128)}) custom-call(f32[8,160]{1,0:T(8,128)S(1)} %copy-done.20, bf16[512,256]{1,0:T(8,128)(2,1)S(1)} %copy-done.19, bf16[512,256]{1,0:T(8,128)(2,1)S(1)} %copy-done.17, bf16[512,1024]{1,0:T(8,128)(2,1)S(1)} %copy-done.9, ...), custom_call_target="tpu_custom_call" | custom-call | flops 21474836480 | bytes 6147072 | tf_op jit(solution)/shard_map/local_grad_kernel/pallas_call | solution.py:489
  330.6 8.1 %grad_state_kernel.1 = (bf16[8,160,128]{2,1,0:T(8,128)(2,1)S(1)}, f32[8,8,160]{2,1,0:T(8,128)S(1)}) custom-call(f32[8,160]{1,0:T(8,128)S(1)} %copy-done.20, bf16[512,256]{1,0:T(8,128)(2,1)S(1)} %copy-done.19, bf16[512,1024]{1,0:T(8,128)(2,1)S(1)} %copy-done.26, bf16[512,1024]{1,0:T(8,128)(2,1)S(1)} %copy-done.11, f32[512,1024]{1,0:T(8,128)S(1)} %copy-done.22, ...), custom_call_target="tpu_custom_call" | custom-call | flops 2684354560 | bytes 4463616 | tf_op jit(solution)/shard_map/grad_state_kernel/pallas_call | solution.py:489
  366.5 8.9 %collective-permute-done.67 = f32[8,8,160]{2,1,0:T(8,128)S(1)} collective-permute-done((f32[8,8,160]{2,1,0:T(8,128)S(1)}, f32[8,8,160]{2,1,0:T(8,128)S(1)}, u32[]{:S(2)}, u32[]{:S(2)}) %collective-permute-start.67) | collective-permute-done | bytes 40992 | tf_op jit(solution)/shard_map/ppermute | solution.py:32
  389.4 6.0 collective-permute-done.65
  399.0 11.2 %finish_grad_kernel.1 = (bf16[512,256]{1,0:T(8,128)(2,1)S(1)}, bf16[512,1024]{1,0:T(8,128)(2,1)S(1)}) custom-call(f32[8,160]{1,0:T(8,128)S(1)} %copy-done.20, bf16[512,256]{1,0:T(8,128)(2,1)S(1)} %copy-done.17, bf16[512,1024]{1,0:T(8,128)(2,1)S(1)} %copy-done.9, f32[512,256]{1,0:T(8,128)S(1)} %get-tuple-element.31.dk_in_ref, f32[512,1024]{1,0:T(8,128)S(1)} %copy-done.27, ...), custom_call_target="tpu_custom_call" | custom-call | flops 5368709120 | bytes 4307968 | tf_op jit(solution)/shard_map/finish_grad_kernel/pallas_call | solution.py:489
  432.0 5.1 collective-permute-done.87
  474.5 34.2 %collective-permute-done.79 = bf16[256,1536]{1,0:T(8,128)(2,1)} collective-permute-done((bf16[256,1536]{1,0:T(8,128)(2,1)}, bf16[256,1536]{1,0:T(8,128)(2,1)}, u32[]{:S(2)}, u32[]{:S(2)}) %collective-permute-start.79) | collective-permute-done | bytes 786464 | tf_op jit(solution)/shard_map/ppermute | solution.py:32
  523.3 15.0 %collective-permute-done.100 = bf16[512,1376]{0,1:T(8,128)(2,1)} collective-permute-done((bf16[512,1376]{0,1:T(8,128)(2,1)}, bf16[512,1376]{0,1:T(8,128)(2,1)}, u32[]{:S(2)}, u32[]{:S(2)}) %collective-permute-start.100) | collective-permute-done | bytes 1409056 | tf_op jit(solution)/shard_map/ppermute | solution.py:32
  538.3 4.3 add_convert_fusion.2
  560.8 14.1 %collective-permute-done.82 = bf16[32,1536]{1,0:T(8,128)(2,1)S(1)} collective-permute-done((bf16[32,1536]{1,0:T(8,128)(2,1)S(1)}, bf16[32,1536]{1,0:T(8,128)(2,1)S(1)}, u32[]{:S(2)}, u32[]{:S(2)}) %collective-permute-start.82) | collective-permute-done | bytes 98336 | tf_op jit(solution)/shard_map/ppermute | solution.py:27
  577.1 15.8 %collective-permute-done.109 = bf16[2,64,1376]{2,1,0:T(8,128)(2,1)S(1)} collective-permute-done((bf16[2,64,1376]{2,1,0:T(8,128)(2,1)S(1)}, bf16[2,64,1376]{2,1,0:T(8,128)(2,1)S(1)}, u32[]{:S(2)}, u32[]{:S(2)}) %collective-permute-start.109) | collective-permute-done | bytes 352288 | tf_op jit(solution)/shard_map/ppermute | solution.py:27
  610.2 5.4 collective-permute-start.102
  615.6 9.2 %collective-permute-done.96 = bf16[64,1376]{1,0:T(8,128)(2,1)S(1)} collective-permute-done((bf16[64,1376]{1,0:T(8,128)(2,1)S(1)}, bf16[64,1376]{1,0:T(8,128)(2,1)S(1)}, u32[]{:S(2)}, u32[]{:S(2)}) %collective-permute-start.96) | collective-permute-done | bytes 176160 | tf_op jit(solution)/shard_map/ppermute | solution.py:27
  625.5 5.7 collective-permute-done.103
  (553 shorter events, 308.5 us)
Async XLA Ops:
  8.6 48.7 %collective-permute-start.27 = (bf16[32,1024]{1,0:T(8,128)(2,1)}, bf16[32,1024]{1,0:T(8,128)(2,1)S(1)}, u32[]{:S(2)}, u32[]{:S(2)}) collective-permute-start(bf16[32,1024]{1,0:T(8,128)(2,1)} %param.19), channel_id=1, source_target_pairs={{0,12},{1,13},{2,14},{3,15},{4,8},{5,9},{6,10},{7,11},{8,4},{9,5},... | collective-permute-start | bytes 196616 | tf_op jit(solution)/shard_map/ppermute | solution.py:27
  12.5 46.2 %collective-permute-start.26 = (bf16[32,1024]{1,0:T(8,128)(2,1)}, bf16[32,1024]{1,0:T(8,128)(2,1)S(1)}, u32[]{:S(2)}, u32[]{:S(2)}) collective-permute-start(bf16[32,1024]{1,0:T(8,128)(2,1)} %param.19), channel_id=1, source_target_pairs={{0,8},{1,9},{2,10},{3,11},{4,12},{5,13},{6,14},{7,15},{8,0},{9,1},... | collective-permute-start | bytes 196616 | tf_op jit(solution)/shard_map/ppermute | solution.py:27
  28.4 45.6 %collective-permute-start.9 = (bf16[4,32,1536]{2,1,0:T(8,128)(2,1)S(1)}, bf16[4,32,1536]{2,1,0:T(8,128)(2,1)S(1)}, u32[]{:S(2)}, u32[]{:S(2)}) collective-permute-start(bf16[4,32,1536]{2,1,0:T(8,128)(2,1)S(1)} %pad_maximum_fusion.3.refs_0_), channel_id=1, source_target_pairs={{0,16},{16,0},{1,17},{17,1},{2,18},{18,2},{3,19},{19,3},{4,20},{20... | collective-permute-start | bytes 1179656 | tf_op jit(solution)/shard_map/ppermute | solution.py:32
  29.9 44.7 %collective-permute-start.10 = (bf16[4,32,1536]{2,1,0:T(8,128)(2,1)S(1)}, bf16[4,32,1536]{2,1,0:T(8,128)(2,1)S(1)}, u32[]{:S(2)}, u32[]{:S(2)}) collective-permute-start(bf16[4,32,1536]{2,1,0:T(8,128)(2,1)S(1)} %collective-permute-done.8.refs_1_), channel_id=1, source_target_pairs={{0,16},{16,0},{1,17},{17,1},{2,18},{18,2},{3,19},{19,3},{4,20},{20... | collective-permute-start | bytes 1179656 | tf_op jit(solution)/shard_map/ppermute | solution.py:32
  79.9 28.9 %collective-permute-start.36 = (bf16[64,1376]{1,0:T(8,128)(2,1)S(1)}, bf16[64,1376]{1,0:T(8,128)(2,1)S(1)}, u32[]{:S(2)}, u32[]{:S(2)}) collective-permute-start(bf16[64,1376]{1,0:T(8,128)(2,1)S(1)} %copy-done.73), channel_id=1, source_target_pairs={{0,8},{1,9},{2,10},{3,11},{4,12},{5,13},{6,14},{7,15},{8,0},{9,1},... | collective-permute-start | bytes 528392 | tf_op jit(solution)/shard_map/ppermute | solution.py:27
  81.5 37.0 %collective-permute-start.28 = (bf16[4,32,1024]{2,1,0:T(8,128)(2,1)S(1)}, bf16[4,32,1024]{2,1,0:T(8,128)(2,1)S(1)}, u32[]{:S(2)}, u32[]{:S(2)}) collective-permute-start(bf16[4,32,1024]{2,1,0:T(8,128)(2,1)S(1)} %pad_maximum_fusion.5.refs_0_), channel_id=1, source_target_pairs={{0,2},{1,3},{2,0},{3,1},{4,6},{5,7},{6,4},{7,5},{8,10},{9,11},{10,... | collective-permute-start | bytes 786440 | tf_op jit(solution)/shard_map/ppermute | solution.py:27
  118.5 33.1 %collective-permute-start.49 = (bf16[2,64,1376]{2,1,0:T(8,128)(2,1)S(1)}, bf16[2,64,1376]{2,1,0:T(8,128)(2,1)S(1)}, u32[]{:S(2)}, u32[]{:S(2)}) collective-permute-start(bf16[2,64,1376]{2,1,0:T(8,128)(2,1)S(1)} %get-tuple-element.76), channel_id=1, source_target_pairs={{0,8},{1,9},{2,10},{3,11},{4,12},{5,13},{6,14},{7,15},{8,0},{9,1},... | collective-permute-start | bytes 1056776 | tf_op jit(solution)/shard_map/ppermute | solution.py:27
  120.4 31.8 %collective-permute-start.48 = (bf16[2,64,1376]{2,1,0:T(8,128)(2,1)S(1)}, bf16[2,64,1376]{2,1,0:T(8,128)(2,1)S(1)}, u32[]{:S(2)}, u32[]{:S(2)}) collective-permute-start(bf16[2,64,1376]{2,1,0:T(8,128)(2,1)S(1)} %get-tuple-element.76), channel_id=1, source_target_pairs={{0,4},{1,5},{2,6},{3,7},{4,0},{5,1},{6,2},{7,3},{8,12},{9,13},{10,... | collective-permute-start | bytes 1056776 | tf_op jit(solution)/shard_map/ppermute | solution.py:27
  121.6 33.9 %collective-permute-start.30 = (bf16[4,32,1024]{2,1,0:T(8,128)(2,1)S(1)}, bf16[4,32,1024]{2,1,0:T(8,128)(2,1)S(1)}, u32[]{:S(2)}, u32[]{:S(2)}) collective-permute-start(bf16[4,32,1024]{2,1,0:T(8,128)(2,1)S(1)} %collective-permute-done.28.refs_1_), channel_id=1, source_target_pairs={{0,16},{16,0},{1,17},{17,1},{2,18},{18,2},{3,19},{19,3},{4,20},{20... | collective-permute-start | bytes 786440 | tf_op jit(solution)/shard_map/ppermute | solution.py:32
  122.2 46.3 %collective-permute-start.16 = (bf16[8,160,128]{2,1,0:T(8,128)(2,1)S(1)}, bf16[8,160,128]{2,1,0:T(8,128)(2,1)S(1)}, u32[]{:S(2)}, u32[]{:S(2)}) collective-permute-start(bf16[8,160,128]{2,1,0:T(8,128)(2,1)S(1)} %fusion.49), channel_id=1, source_target_pairs={{0,1},{1,0},{2,3},{3,2},{4,5},{5,4},{6,7},{7,6},{8,9},{9,8},{10,11... | collective-permute-start | bytes 983048 | tf_op jit(solution)/shard_map/ppermute | solution.py:27
  130.4 57.9 %collective-permute-start.44 = (bf16[4,64,1376]{2,1,0:T(8,128)(2,1)S(1)}, bf16[4,64,1376]{2,1,0:T(8,128)(2,1)}, u32[]{:S(2)}, u32[]{:S(2)}) collective-permute-start(bf16[4,64,1376]{2,1,0:T(8,128)(2,1)S(1)} %pad_maximum_fusion.2.refs_0_), channel_id=1, source_target_pairs={{0,2},{1,3},{2,0},{3,1},{4,6},{5,7},{6,4},{7,5},{8,10},{9,11},{10,... | collective-permute-start | bytes 2113544 | tf_op jit(solution)/shard_map/ppermute | solution.py:27
  151.6 37.3 %collective-permute-start.38 = (bf16[4,64,1376]{2,1,0:T(8,128)(2,1)}, bf16[4,64,1376]{2,1,0:T(8,128)(2,1)}, u32[]{:S(2)}, u32[]{:S(2)}) collective-permute-start(bf16[4,64,1376]{2,1,0:T(8,128)(2,1)} %pad_maximum_fusion.1.refs_0_), channel_id=1, source_target_pairs={{0,2},{1,3},{2,0},{3,1},{4,6},{5,7},{6,4},{7,5},{8,10},{9,11},{10,... | collective-permute-start | bytes 2113544 | tf_op jit(solution)/shard_map/ppermute | solution.py:27
  201.2 35.9 %collective-permute-start.54 = (bf16[4,64,1376]{2,1,0:T(8,128)(2,1)}, bf16[4,64,1376]{2,1,0:T(8,128)(2,1)}, u32[]{:S(2)}, u32[]{:S(2)}) collective-permute-start(bf16[4,64,1376]{2,1,0:T(8,128)(2,1)} %pad_maximum_fusion.1.refs_0_), channel_id=1, source_target_pairs={{0,16},{16,0},{1,17},{17,1},{2,18},{18,2},{3,19},{19,3},{4,20},{20... | collective-permute-start | bytes 2113544 | tf_op jit(solution)/shard_map/ppermute | solution.py:32
  206.4 33.7 %collective-permute-start.51 = (bf16[4,2,64,1376]{3,2,1,0:T(8,128)(2,1)S(1)}, bf16[4,2,64,1376]{3,2,1,0:T(8,128)(2,1)S(1)}, u32[]{:S(2)}, u32[]{:S(2)}) collective-permute-start(bf16[4,2,64,1376]{3,2,1,0:T(8,128)(2,1)S(1)} %pad_maximum_fusion.refs_0_), channel_id=1, source_target_pairs={{0,2},{1,3},{2,0},{3,1},{4,6},{5,7},{6,4},{7,5},{8,10},{9,11},{10,... | collective-permute-start | bytes 4227080 | tf_op jit(solution)/shard_map/ppermute | solution.py:27
  206.4 37.6 %collective-permute-start.59 = (bf16[4,64,1376]{2,1,0:T(8,128)(2,1)}, bf16[4,64,1376]{2,1,0:T(8,128)(2,1)}, u32[]{:S(2)}, u32[]{:S(2)}) collective-permute-start(bf16[4,64,1376]{2,1,0:T(8,128)(2,1)} %collective-permute-done.44.refs_1_), channel_id=1, source_target_pairs={{0,16},{16,0},{1,17},{17,1},{2,18},{18,2},{3,19},{19,3},{4,20},{20... | collective-permute-start | bytes 2113544 | tf_op jit(solution)/shard_map/ppermute | solution.py:32
  212.1 40.4 %collective-permute-start.55 = (bf16[4,64,1376]{2,1,0:T(8,128)(2,1)}, bf16[4,64,1376]{2,1,0:T(8,128)(2,1)}, u32[]{:S(2)}, u32[]{:S(2)}) collective-permute-start(bf16[4,64,1376]{2,1,0:T(8,128)(2,1)} %collective-permute-done.38.refs_1_), channel_id=1, source_target_pairs={{0,16},{16,0},{1,17},{17,1},{2,18},{18,2},{3,19},{19,3},{4,20},{20... | collective-permute-start | bytes 2113544 | tf_op jit(solution)/shard_map/ppermute | solution.py:32
  213.0 31.6 %collective-permute-start.60 = (bf16[4,64,1376]{2,1,0:T(8,128)(2,1)}, bf16[4,64,1376]{2,1,0:T(8,128)(2,1)}, u32[]{:S(2)}, u32[]{:S(2)}) collective-permute-start(bf16[4,64,1376]{2,1,0:T(8,128)(2,1)} %collective-permute-done.58.refs_0_), channel_id=1, source_target_pairs={{0,1},{1,0},{2,3},{3,2},{4,5},{5,4},{6,7},{7,6},{8,9},{9,8},{10,11... | collective-permute-start | bytes 2113544 | tf_op jit(solution)/shard_map/ppermute | solution.py:27
  366.5 30.3 %collective-permute-start.85 = (bf16[256,1024]{1,0:T(8,128)(2,1)S(1)}, bf16[256,1024]{1,0:T(8,128)(2,1)S(1)}, u32[]{:S(2)}, u32[]{:S(2)}) collective-permute-start(bf16[256,1024]{1,0:T(8,128)(2,1)S(1)} %convolution_convert_fusion.18), channel_id=1, source_target_pairs={{0,1},{1,0},{2,3},{3,2},{4,5},{5,4},{6,7},{7,6},{8,9},{9,8},{10,11... | collective-permute-start | bytes 1572872 | tf_op jit(solution)/shard_map/ppermute | solution.py:27
  385.0 40.3 %collective-permute-start.84 = (bf16[256,1024]{1,0:T(8,128)(2,1)}, bf16[256,1024]{1,0:T(8,128)(2,1)}, u32[]{:S(2)}, u32[]{:S(2)}) collective-permute-start(bf16[256,1024]{1,0:T(8,128)(2,1)} %convolution_convert_fusion.20), channel_id=1, source_target_pairs={{0,1},{1,0},{2,3},{3,2},{4,5},{5,4},{6,7},{7,6},{8,9},{9,8},{10,11... | collective-permute-start | bytes 1572872 | tf_op jit(solution)/shard_map/ppermute | solution.py:27
  385.1 66.1 %collective-permute-start.92 = (bf16[512,1376]{0,1:T(8,128)(2,1)}, bf16[512,1376]{0,1:T(8,128)(2,1)}, u32[]{:S(2)}, u32[]{:S(2)}) collective-permute-start(bf16[512,1376]{0,1:T(8,128)(2,1)} %convolution_convert_fusion.8), channel_id=1, source_target_pairs={{0,1},{1,0},{2,3},{3,2},{4,5},{5,4},{6,7},{7,6},{8,9},{9,8},{10,11... | collective-permute-start | bytes 4227080 | tf_op jit(solution)/shard_map/ppermute | solution.py:27
  395.4 59.9 %collective-permute-start.105 = (bf16[512,1376]{0,1:T(8,128)(2,1)}, bf16[512,1376]{0,1:T(8,128)(2,1)}, u32[]{:S(2)}, u32[]{:S(2)}) collective-permute-start(bf16[512,1376]{0,1:T(8,128)(2,1)} %convolution_convert_fusion.2), channel_id=1, source_target_pairs={{0,1},{1,0},{2,3},{3,2},{4,5},{5,4},{6,7},{7,6},{8,9},{9,8},{10,11... | collective-permute-start | bytes 4227080 | tf_op jit(solution)/shard_map/ppermute | solution.py:27
  398.1 29.1 %collective-permute-start.86 = (bf16[256,1024]{1,0:T(8,128)(2,1)}, bf16[256,1024]{1,0:T(8,128)(2,1)}, u32[]{:S(2)}, u32[]{:S(2)}) collective-permute-start(bf16[256,1024]{1,0:T(8,128)(2,1)} %add_convert_fusion.13), channel_id=1, source_target_pairs={{0,16},{16,0},{1,17},{17,1},{2,18},{18,2},{3,19},{19,3},{4,20},{20... | collective-permute-start | bytes 1572872 | tf_op jit(solution)/shard_map/ppermute | solution.py:32
  425.2 35.7 %collective-permute-start.106 = (bf16[512,1376]{0,1:T(8,128)(2,1)}, bf16[512,1376]{0,1:T(8,128)(2,1)}, u32[]{:S(2)}, u32[]{:S(2)}) collective-permute-start(bf16[512,1376]{0,1:T(8,128)(2,1)} %convolution_convert_fusion), channel_id=1, source_target_pairs={{0,1},{1,0},{2,3},{3,2},{4,5},{5,4},{6,7},{7,6},{8,9},{9,8},{10,11... | collective-permute-start | bytes 4227080 | tf_op jit(solution)/shard_map/ppermute | solution.py:27
  447.2 65.9 %collective-permute-start.91 = (bf16[512,1376]{0,1:T(8,128)(2,1)}, bf16[512,1376]{0,1:T(8,128)(2,1)}, u32[]{:S(2)}, u32[]{:S(2)}) collective-permute-start(bf16[512,1376]{0,1:T(8,128)(2,1)} %convolution_convert_fusion.10), channel_id=1, source_target_pairs={{0,1},{1,0},{2,3},{3,2},{4,5},{5,4},{6,7},{7,6},{8,9},{9,8},{10,11... | collective-permute-start | bytes 4227080 | tf_op jit(solution)/shard_map/ppermute | solution.py:27
  457.7 55.7 %collective-permute-start.93 = (bf16[512,1376]{0,1:T(8,128)(2,1)}, bf16[512,1376]{0,1:T(8,128)(2,1)}, u32[]{:S(2)}, u32[]{:S(2)}) collective-permute-start(bf16[512,1376]{0,1:T(8,128)(2,1)} %add_convert_fusion.6), channel_id=1, source_target_pairs={{0,16},{16,0},{1,17},{17,1},{2,18},{18,2},{3,19},{19,3},{4,20},{20... | collective-permute-start | bytes 4227080 | tf_op jit(solution)/shard_map/ppermute | solution.py:32
  460.8 47.9 %collective-permute-start.79 = (bf16[256,1536]{1,0:T(8,128)(2,1)}, bf16[256,1536]{1,0:T(8,128)(2,1)}, u32[]{:S(2)}, u32[]{:S(2)}) collective-permute-start(bf16[256,1536]{1,0:T(8,128)(2,1)} %add_convert_fusion.10), channel_id=1, source_target_pairs={{0,16},{16,0},{1,17},{17,1},{2,18},{18,2},{3,19},{19,3},{4,20},{20... | collective-permute-start | bytes 2359304 | tf_op jit(solution)/shard_map/ppermute | solution.py:32
  468.9 54.4 %collective-permute-start.98 = (bf16[512,1376]{0,1:T(8,128)(2,1)}, bf16[512,1376]{0,1:T(8,128)(2,1)}, u32[]{:S(2)}, u32[]{:S(2)}) collective-permute-start(bf16[512,1376]{0,1:T(8,128)(2,1)} %convolution_convert_fusion.6), channel_id=1, source_target_pairs={{0,1},{1,0},{2,3},{3,2},{4,5},{5,4},{6,7},{7,6},{8,9},{9,8},{10,11... | collective-permute-start | bytes 4227080 | tf_op jit(solution)/shard_map/ppermute | solution.py:27
  473.0 65.3 %collective-permute-start.100 = (bf16[512,1376]{0,1:T(8,128)(2,1)}, bf16[512,1376]{0,1:T(8,128)(2,1)}, u32[]{:S(2)}, u32[]{:S(2)}) collective-permute-start(bf16[512,1376]{0,1:T(8,128)(2,1)} %add_convert_fusion.3), channel_id=1, source_target_pairs={{0,16},{16,0},{1,17},{17,1},{2,18},{18,2},{3,19},{19,3},{4,20},{20... | collective-permute-start | bytes 4227080 | tf_op jit(solution)/shard_map/ppermute | solution.py:32
  508.7 39.5 %collective-permute-start.107 = (bf16[4,2,64,1376]{3,2,0,1:T(8,128)(2,1)}, bf16[4,2,64,1376]{3,2,0,1:T(8,128)(2,1)}, u32[]{:S(2)}, u32[]{:S(2)}) collective-permute-start(bf16[4,2,64,1376]{3,2,0,1:T(8,128)(2,1)} %fusion.27), channel_id=1, source_target_pairs={{0,2},{1,3},{2,0},{3,1},{4,6},{5,7},{6,4},{7,5},{8,10},{9,11},{10,... | collective-permute-start | bytes 4227080 | tf_op jit(solution)/shard_map/ppermute | solution.py:27
  513.1 38.9 %collective-permute-start.80 = (bf16[4,32,1536]{2,1,0:T(8,128)(2,1)S(1)}, bf16[4,32,1536]{2,1,0:T(8,128)(2,1)}, u32[]{:S(2)}, u32[]{:S(2)}) collective-permute-start(bf16[4,32,1536]{2,1,0:T(8,128)(2,1)S(1)} %dynamic-slice_bitcast_fusion.2), channel_id=1, source_target_pairs={{0,2},{1,3},{2,0},{3,1},{4,6},{5,7},{6,4},{7,5},{8,10},{9,11},{10,... | collective-permute-start | bytes 1179656 | tf_op jit(solution)/shard_map/ppermute | solution.py:27
  521.6 77.9 %collective-permute-start.94 = (bf16[4,64,1376]{2,1,0:T(8,128)(2,1)}, bf16[4,64,1376]{2,1,0:T(8,128)(2,1)}, u32[]{:S(2)}, u32[]{:S(2)}) collective-permute-start(bf16[4,64,1376]{2,1,0:T(8,128)(2,1)} %dynamic-slice_bitcast_fusion.1), channel_id=1, source_target_pairs={{0,2},{1,3},{2,0},{3,1},{4,6},{5,7},{6,4},{7,5},{8,10},{9,11},{10,... | collective-permute-start | bytes 2113544 | tf_op jit(solution)/shard_map/ppermute | solution.py:27
  546.4 58.9 %collective-permute-start.101 = (bf16[4,64,1376]{2,1,0:T(8,128)(2,1)S(1)}, bf16[4,64,1376]{2,1,0:T(8,128)(2,1)S(1)}, u32[]{:S(2)}, u32[]{:S(2)}) collective-permute-start(bf16[4,64,1376]{2,1,0:T(8,128)(2,1)S(1)} %dynamic-slice_bitcast_fusion), channel_id=1, source_target_pairs={{0,2},{1,3},{2,0},{3,1},{4,6},{5,7},{6,4},{7,5},{8,10},{9,11},{10,... | collective-permute-start | bytes 2113544 | tf_op jit(solution)/shard_map/ppermute | solution.py:27
  (179 other events, 2216.8 us)

commit v2 on v1

--- a/solution.py
+++ b/solution.py
@@ -580,6 +580,525 @@
     return narrow(result)
 
 
+MESH = pl.DeviceIdType.MESH
+GAIN_COLS = 128
+
+
+class Links:
+    def __init__(self):
+        self.head, self.seq = lax.axis_index("head"), lax.axis_index("seq")
+        self.n = lax.axis_size("seq")
+        self.z, self.y, self.c = self.seq // 4, (self.seq // 2) % 2, self.seq % 2
+        self.core = self.at(self.head, self.seq ^ 1)
+        self.x = self.at(1 - self.head, self.seq)
+        self.near = self.at(self.head, self.seq ^ 2)
+        self.far = [self.at(self.head, self.seq ^ (4 * r)) for r in range(4)]
+
+    def at(self, head, seq):
+        return {"head": head, "seq": seq}
+
+    def shifted(self, distance):
+        return self.at(self.head, lax.rem(self.seq + distance + self.n, self.n))
+
+    def greet(self):
+        barrier = pltpu.get_barrier_semaphore()
+        partners = [self.core, self.x, self.near] + self.far[1:]
+        partners += [self.shifted(d) for d in (2, 4, -2, -4)]
+        for partner in partners:
+            pl.semaphore_signal(barrier, inc=1, device_id=partner, device_id_type=MESH)
+        pl.semaphore_wait(barrier, len(partners))
+
+
+class Copies:
+    def __init__(self, send, recv, local):
+        self.send, self.recv, self.local = send, recv, local
+        self.used, self.used_local = 0, 0
+        self.started, self.started_local = [], []
+
+    def remote(self, src, dst, partner):
+        i = self.used
+        self.used += 1
+        return pltpu.make_async_remote_copy(
+            src_ref=src,
+            dst_ref=dst,
+            send_sem=self.send.at[i],
+            recv_sem=self.recv.at[i],
+            device_id=partner,
+            device_id_type=MESH,
+        )
+
+    def go(self, *copies):
+        for copy in copies:
+            copy.start()
+            self.started.append(copy)
+
+    def keep(self, src, dst):
+        copy = pltpu.make_async_copy(src, dst, self.local.at[self.used_local])
+        self.used_local += 1
+        copy.start()
+        self.started_local.append(copy)
+        return copy
+
+    def drain(self):
+        for copy in self.started:
+            copy.wait_send()
+        for copy in self.started_local:
+            copy.wait()
+
+
+def arrived(*copies):
+    for copy in copies:
+        copy.wait_recv()
+
+
+class WideGather:
+    def __init__(self, copies, links, shard, own, other, other_there):
+        n, y, c = links, links.y, links.c
+        self.copies = copies
+        self.place = own.at[n.z, y, c]
+        self.shard = shard
+        self.far = [copies.remote(shard, self.place, n.far[r]) for r in range(1, 4)]
+        mine, theirs = own.at[:, y, c], own.at[:, 1 - y, c]
+        self.near = copies.remote(mine, mine, n.near)
+        self.cross = [
+            copies.remote(mine, other_there.at[:, y, c], n.x),
+            copies.remote(theirs, other_there.at[:, 1 - y, c], n.x),
+        ]
+        self.core = [
+            copies.remote(part, part, n.core)
+            for part in (mine, theirs, other.at[:, y, c], other.at[:, 1 - y, c])
+        ]
+
+    def begin(self):
+        self.copies.go(*self.far)
+        self.own = self.copies.keep(self.shard, self.place)
+
+    def one(self):
+        arrived(*self.far)
+        self.own.wait()
+        self.copies.started_local.remove(self.own)
+        self.copies.go(self.near, self.cross[0], self.core[0])
+
+    def two(self):
+        arrived(self.near)
+        self.copies.go(self.cross[1], self.core[1])
+
+    def three(self):
+        arrived(self.cross[0])
+        self.copies.go(self.core[2])
+
+    def four(self):
+        arrived(self.cross[1])
+        self.copies.go(self.core[3])
+
+    def end(self):
+        arrived(*self.core)
+
+
+class TallGather:
+    def __init__(self, copies, links, shard, own, other):
+        n, y, c = links, links.y, links.c
+        self.copies = copies
+        self.shard, self.place = shard, own.at[n.z, y, c]
+        received = other.at[n.z, y, c]
+        self.cross = copies.remote(shard, received, n.x)
+        self.far_own = [copies.remote(shard, self.place, n.far[r]) for r in range(1, 4)]
+        self.far_other = [copies.remote(received, received, n.far[r]) for r in range(1, 4)]
+        mine = [own.at[:, y, c], other.at[:, y, c]]
+        theirs = [own.at[:, 1 - y, c], other.at[:, 1 - y, c]]
+        self.near = [copies.remote(part, part, n.near) for part in mine]
+        self.core = [copies.remote(part, part, n.core) for part in mine + theirs]
+
+    def begin(self):
+        self.copies.go(self.cross)
+        self.own = self.copies.keep(self.shard, self.place)
+
+    def zero(self):
+        self.copies.go(*self.far_own)
+        arrived(self.cross)
+        self.copies.go(*self.far_other)
+
+    def one(self):
+        arrived(*self.far_own)
+        self.own.wait()
+        self.copies.started_local.remove(self.own)
+        self.copies.go(self.near[0], self.core[0])
+
+    def two(self):
+        arrived(*self.far_other)
+        self.copies.go(self.near[1], self.core[1])
+
+    def three(self):
+        arrived(self.near[0])
+        self.copies.go(self.core[2])
+
+    def four(self):
+        arrived(self.near[1])
+        self.copies.go(self.core[3])
+
+    def end(self):
+        arrived(*self.core)
+
+
+class Exchange:
+    def __init__(self, copies, links, gates, first, bufs, forward):
+        n = links
+        self.copies, self.gates, self.first, self.bufs = copies, gates, first, bufs
+        half = PAIRS // 2
+        step = 2 if forward else -2
+        own, a, j, b, j2, r1, r2, far = bufs
+
+        def both(src, dst, partner):
+            return [copies.remote(s, d, partner) for s, d in zip(src, dst)]
+
+        def halves(state):
+            return [
+                state[0].at[pl.ds(n.c * half, half)],
+                state[1].at[pl.ds(n.c * half, half)],
+            ]
+
+        self.rounds = [
+            both(own, a, n.x),
+            both(j, b, n.core),
+            both(halves(j2), r1, n.shifted(step)) + both(halves(j2), r2, n.shifted(2 * step)),
+            both(halves(far), halves(far), n.core),
+        ]
+        self.halves = halves
+        self.total = None
+
+    def gate(self, i):
+        return self.gates[self.first + i]
+
+    def begin(self):
+        self.copies.go(*self.rounds[0])
+
+    def one(self):
+        own, a, j, b, j2, r1, r2, far = self.bufs
+        arrived(*self.rounds[0])
+        for s, d, t in zip(own, a, j):
+            t[...] = (
+                s[...].astype(F32) * self.gate(1) + d[...].astype(F32) * self.gate(2)
+            ).astype(t.dtype)
+        self.copies.go(*self.rounds[1])
+
+    def two(self):
+        own, a, j, b, j2, r1, r2, far = self.bufs
+        arrived(*self.rounds[1])
+        for s, d, t in zip(j, b, j2):
+            t[...] = (
+                s[...].astype(F32) * self.gate(4) + d[...].astype(F32) * self.gate(5)
+            ).astype(t.dtype)
+        self.copies.go(*self.rounds[2])
+
+    def three(self):
+        own, a, j, b, j2, r1, r2, far = self.bufs
+        arrived(*self.rounds[2])
+        for s, d, t in zip(r1, r2, self.halves(far)):
+            t[...] = (s[...].astype(F32) + d[...].astype(F32) * self.gate(6)).astype(t.dtype)
+        self.copies.go(*self.rounds[3])
+
+    def four(self, out):
+        own, a, j, b, j2, r1, r2, far = self.bufs
+        arrived(*self.rounds[3])
+        for s, d, f, t in zip(a, b, far, out):
+            t[...] = (
+                s[...].astype(F32) * self.gate(0)
+                + d[...].astype(F32) * self.gate(3)
+                + f[...].astype(F32) * self.gate(7)
+            ).astype(t.dtype)
+
+
+def exchange_shapes():
+    shapes = []
+    for name in range(8):
+        pairs = PAIRS // 2 if name in (5, 6) else PAIRS
+        shapes += [pltpu.VMEM((pairs, FEATS, WIDE), BF), pltpu.VMEM((pairs, 8, FEATS), F32)]
+    return shapes
+
+
+def exchange_gates(ids, rows, forward):
+    head, seq = lax.axis_index("head"), lax.axis_index("seq")
+    n = lax.axis_size("seq")
+    segments = 2 * n
+    ends = ids.reshape(segments, rows)
+    firsts, lasts = ends[:, 0], ends[:, rows - 1]
+    step = 1 if forward else -1
+    near_end, far_end = (lasts, firsts) if forward else (firsts, lasts)
+    seg = 2 * seq + head
+    base = 4 * (seq // 2)
+    core = seq % 2
+    late_head = (head == 1) if forward else (head == 0)
+    late_core = (core == 1) if forward else (core == 0)
+    pair_early, pair_late = (2 * seq, 2 * seq + 1) if forward else (2 * seq + 1, 2 * seq)
+    early_end, late_end = (base + 1, base + 3) if forward else (base + 2, base)
+    chip = seq // 2
+    near_ok = (chip >= 1) if forward else (chip < n // 2 - 1)
+    far_ok = (chip >= 2) if forward else (chip < n // 2 - 2)
+    where = jnp.stack(
+        [seg - step, pair_early, pair_late, early_end, late_end, late_end - 4 * step,
+         late_end - 8 * step]
+    )
+    docs = near_end[jnp.clip(where, 0, segments - 1)]
+    takes = far_end[seg]
+    joined = docs[1] == docs[2]
+    joined2 = docs[3] == docs[4]
+    flags = [
+        late_head & (docs[0] == takes),
+        late_head | joined,
+        (~late_head) | joined,
+        late_core & (docs[3] == takes),
+        late_core | joined2,
+        (~late_core) | joined2,
+        far_ok & (docs[5] == docs[6]),
+        near_ok & (docs[5] == takes),
+    ]
+    return jnp.stack(flags).astype(F32)
+
+
+def pair_lanes(pair, start=0):
+    return pl.ds(pl.multiple_of(start + pair * WIDE, WIDE), WIDE)
+
+
+def state_pair(pair, table, keys, value, last, wide_ref, thin_ref):
+    rows = keys.shape[0]
+    total = None
+    for part in range(2):
+        sel = selectors(table, 2 * pair + part)
+        one, two = factors(keys, table, sel)
+        phi = one * two * last
+        new = mm(phi.astype(BF), keep(half_mask(rows, part), value), TN)
+        total = new if total is None else total + new
+        thin_ref[pair, part : part + 1, :] = jnp.sum(phi, axis=0, keepdims=True)
+    thin_ref[pair, 2:, :] = jnp.zeros((6, FEATS), F32)
+    wide_ref[pair] = total.astype(BF)
+
+
+def local_pair(pair, qkv, num_ref, den_ref, mask_ref):
+    rows = qkv.shape[0]
+    qk = HEADS * QD
+    for i in range(rows // TILE):
+        here = slice(i * TILE, (i + 1) * TILE)
+        num = jnp.zeros((TILE, WIDE), F32)
+        dens = []
+        for part in range(2):
+            head = 2 * pair + part
+            query = keep(head_mask(TILE, head), qkv[here, :qk] * (QD**-0.5))
+            den = jnp.zeros((TILE, 1), F32)
+            for j in range(i + 1):
+                there = slice(j * TILE, (j + 1) * TILE)
+                s = mm(query, qkv[there, qk : 2 * qk], NT)
+                w = (1.0 + s + 0.5 * s * s) * mask_ref[here, there]
+                den = den + jnp.sum(w, axis=1, keepdims=True)
+                value = qkv[there, pair_lanes(pair, 2 * qk)]
+                num = num + mm(w.astype(BF), keep(half_mask(TILE, part), value), NN)
+            dens.append(den)
+        num_ref[here, pair_lanes(pair)] = num
+        den_ref[here, pair_lanes(pair)] = jnp.where(half_mask(TILE, 0), dens[0], dens[1])
+
+
+def finish_pair(pair, table, query, first, num_ref, den_ref, wide_ref, thin_ref, out_ref):
+    rows = query.shape[0]
+    lanes = pair_lanes(pair)
+    num, den = num_ref[:, lanes], den_ref[:, lanes]
+    for part in range(2):
+        sel = selectors(table, 2 * pair + part)
+        one, two = factors(query, table, sel)
+        phi = one * two * (table[4:5, :] * first)
+        mask = half_mask(rows, part)
+        num = num + jnp.where(mask, mm(phi.astype(BF), wide_ref[pair], NN), 0.0)
+        more = jnp.sum(phi * thin_ref[pair, part : part + 1, :], axis=1, keepdims=True)
+        den = den + jnp.where(mask, more, 0.0)
+    rden = 1.0 / den
+    den_ref[:, lanes] = rden
+    out_ref[:, lanes] = (num * rden).astype(BF)
+
+
+def each_pair(low, high, step):
+    def one(pair, carry):
+        step(pair)
+        return carry
+
+    lax.fori_loop(low, high, one, 0)
+
+
+WIDE_COPIES, TALL_COPIES, EXCHANGE_COPIES = 10, 15, 10
+FWD_COPIES = 5 * WIDE_COPIES + TALL_COPIES + EXCHANGE_COPIES
+FWD_LOCALS = 20
+
+
+def forward_kernel(
+    x_ref, qs_ref, os_ref, gs_ref, us_ref, ds_ref, row_ids_ref, col_ids_ref, first_ref, last_ref,
+    table_ref, gates_ref,
+    g_own, g_other, u_own, u_other, d_own, d_other, wq_out, wo_out, qkv_out, att_out, rden_out,
+    res_out, n2_out, wide_out, thin_out, gain_out,
+    wq, wo, normed, qkv, num, den, mask, att, res, n2, wide, thin, gain, *rest,
+):
+    bufs, (send, recv, local) = rest[:16], rest[16:]
+    states = [(bufs[2 * i], bufs[2 * i + 1]) for i in range(8)]
+    n = Links()
+    copies = Copies(send, recv, local)
+    rows, width = x_ref.shape
+    qk, hv = HEADS * QD, HEADS * VD
+    cut = 7 * 128
+    full = wq.shape[-1]
+
+    def side(ref, head, lo=None, hi=None):
+        return ref.at[head] if lo is None else ref.at[head, :, :, :, :, pl.ds(lo, hi - lo)]
+
+    q_parts = []
+    for lo, hi in ((0, cut), (cut, full)):
+        shard = qs_ref.at[:, pl.ds(lo, hi - lo)]
+        own, other = side(wq, n.head, lo, hi), side(wq, 1 - n.head, lo, hi)
+        q_parts.append(WideGather(copies, n, shard, own, other, own))
+    own, other = side(wo, n.head), side(wo, 1 - n.head)
+    outs = WideGather(copies, n, os_ref, own, other, own)
+    gates = WideGather(copies, n, gs_ref, g_own, g_other, g_other)
+    ups = WideGather(copies, n, us_ref, u_own, u_other, u_other)
+    downs = TallGather(copies, n, ds_ref, d_own, d_other)
+    swap = Exchange(copies, n, gates_ref, 0, states, True)
+
+    n.greet()
+    for part in q_parts:
+        part.begin()
+    outs.begin()
+    gates.begin()
+    ups.begin()
+    downs.begin()
+
+    table = table_ref[...]
+    x = x_ref[...].astype(F32)
+    scaled = x * lax.rsqrt(jnp.mean(x * x, axis=-1, keepdims=True) + EPSILON)
+    visible_tile(mask, row_ids_ref, col_ids_ref, rows)
+    for part in q_parts:
+        part.one()
+    outs.one()
+    for part in q_parts:
+        part.two()
+        part.three()
+    outs.two()
+    outs.three()
+    for part in q_parts:
+        part.four()
+    downs.zero()
+    for part in q_parts:
+        part.end()
+    outs.four()
+    gates.one()
+
+    pick_gain = (
+        lax.broadcasted_iota(jnp.int32, (8, GAIN_COLS), 0)
+        == lax.broadcasted_iota(jnp.int32, (8, GAIN_COLS), 1)
+    ).astype(F32).astype(BF)
+    gain[...] = mm(pick_gain, wq[..., full - GAIN_COLS :].reshape(width, GAIN_COLS), NT)
+    normed[...] = (scaled * gain[0:1, :]).astype(BF)
+    h1 = normed[...]
+    for lo in range(0, 2 * qk + hv, 256):
+        weight = wq[..., lo : lo + 256].reshape(width, 256)
+        qkv[:, lo : lo + 256] = mm(h1, weight, NN).astype(BF)
+    copies.keep(qkv, qkv_out)
+    copies.keep(wq, wq_out)
+    copies.keep(gain, gain_out)
+
+    def do_state(pair):
+        state_pair(
+            pair, table, qkv[:, qk : 2 * qk], qkv[:, pair_lanes(pair, 2 * qk)], last_ref[...],
+            states[0][0], states[0][1],
+        )
+
+    def do_local(pair):
+        local_pair(pair, qkv, num, den, mask)
+
+    each_pair(0, PAIRS, do_state)
+    swap.begin()
+    outs.end()
+    copies.keep(wo, wo_out)
+    each_pair(0, 3, do_local)
+    swap.one()
+    gates.two()
+    ups.one()
+    each_pair(3, 5, do_local)
+    swap.two()
+    downs.one()
+    gates.three()
+    each_pair(5, PAIRS, do_local)
+    swap.three()
+    ups.two()
+    downs.two()
+    swap.four((wide, thin))
+    copies.keep(wide, wide_out)
+    copies.keep(thin, thin_out)
+
+    def do_finish(pair):
+        finish_pair(
+            pair, table, qkv[:, :qk], first_ref[...], num, den, wide, thin, att
+        )
+
+    each_pair(0, PAIRS, do_finish)
+    gates.four()
+    downs.three()
+    copies.keep(att, att_out)
+    copies.keep(den, rden_out)
+    o = att[...]
+    for lo in range(0, width, 256):
+        weight = wo[..., lo : lo + 256].reshape(hv, 256)
+        res[:, lo : lo + 256] = x_ref[:, lo : lo + 256].astype(F32) + mm(o, weight, NN)
+    copies.keep(res, res_out)
+    y1 = res[...]
+    n2[...] = (
+        y1 * lax.rsqrt(jnp.mean(y1 * y1, axis=-1, keepdims=True) + EPSILON) * gain[1:2, :]
+    ).astype(BF)
+    copies.keep(n2, n2_out)
+    downs.four()
+    ups.three()
+    gates.end()
+    downs.end()
+    ups.four()
+    ups.end()
+    copies.drain()
+
+
+def forward(x, q_shard, o_shard, ffn, row_ids, col_ids, first, last, table, gates):
+    rows, width = x.shape
+    qk, hv = HEADS * QD, HEADS * VD
+    full = q_shard.shape[-1]
+    small, fine, ff = q_shard.shape[0], ffn[0].shape[0], ffn[0].shape[1]
+    half = jax.ShapeDtypeStruct((4, 2, 2, fine, ff), BF)
+    wq_shape, wo_shape = (2, 4, 2, 2, small, full), (2, 4, 2, 2, small, width)
+
+    def like(shape, dtype):
+        return jax.ShapeDtypeStruct(shape, dtype)
+
+    out_shape = [half] * 6 + [
+        like(wq_shape, BF), like(wo_shape, BF), like((rows, 2 * qk + hv), BF),
+        like((rows, hv), BF), like((rows, hv), F32), like((rows, width), F32),
+        like((rows, width), BF), STATE_SHAPES[0], STATE_SHAPES[1], like((8, width), F32),
+    ]
+    scratch = [
+        pltpu.VMEM(wq_shape, BF), pltpu.VMEM(wo_shape, BF), pltpu.VMEM((rows, width), BF),
+        pltpu.VMEM((rows, 2 * qk + hv), BF), pltpu.VMEM((rows, hv), F32),
+        pltpu.VMEM((rows, hv), F32), pltpu.VMEM((rows, rows), F32), pltpu.VMEM((rows, hv), BF),
+        pltpu.VMEM((rows, width), F32), pltpu.VMEM((rows, width), BF),
+        pltpu.VMEM((PAIRS, FEATS, WIDE), BF), pltpu.VMEM((PAIRS, 8, FEATS), F32),
+        pltpu.VMEM((8, width), F32),
+    ] + exchange_shapes() + [
+        pltpu.SemaphoreType.DMA((FWD_COPIES,)), pltpu.SemaphoreType.DMA((FWD_COPIES,)),
+        pltpu.SemaphoreType.DMA((FWD_LOCALS,)),
+    ]
+    vmem = pl.BlockSpec(memory_space=pltpu.VMEM)
+    return pl.pallas_call(
+        forward_kernel,
+        out_shape=out_shape,
+        in_specs=[vmem] * 11 + [pl.BlockSpec(memory_space=pltpu.SMEM)],
+        out_specs=[pl.BlockSpec(memory_space=pl.ANY)] * len(out_shape),
+        scratch_shapes=scratch,
+        compiler_params=pltpu.CompilerParams(
+            collective_id=1, has_side_effects=True, vmem_limit_bytes=56 << 20
+        ),
+        cost_estimate=pl.CostEstimate(flops=8 << 30, bytes_accessed=64 << 20, transcendentals=0),
+        name="forward",
+    )(x, q_shard, o_shard, *ffn, row_ids, col_ids, first, last, table, gates)
+
+
 def rms_scale(values, gain):
     return values * lax.rsqrt(jnp.mean(values * values, axis=-1, keepdims=True) + EPSILON) * gain
 
@@ -616,27 +1135,14 @@
     return [[dot_tn(part, r).astype(BF) for part in out[0]] for r in right]
 
 
-def body(
-    layer_input,
-    segment_ids,
-    norm1_gain,
-    w_query,
-    w_key,
-    w_value,
-    w_out,
-    norm2_gain,
-    w_gate,
-    w_up,
-    w_down,
-    output_grad,
+def plain_forward(
+    inputs, segment_ids, norm1_gain, w_query, w_key, w_value, w_out, norm2_gain, w_gate, w_up,
+    w_down, row_ids, col_ids, first, last, table,
 ):
-    rows = layer_input.shape[1]
     head, seq = lax.axis_index("head"), lax.axis_index("seq")
     n_seq = lax.axis_size("seq")
+    rows, width = inputs.shape
     qk = HEADS * QD
-    inputs = layer_input[0].astype(F32)
-    width = inputs.shape[1]
-
     slot = head * n_seq + seq
     small = norm1_gain.shape[0]
     gains = jnp.zeros((2, width // small, small), F32)
@@ -651,13 +1157,6 @@
     gate_w = gather_halves(w_gate, False)
     up_w = gather_halves(w_up, False)
     down_w = gather_halves(w_down.T, True)
-
-    segment = 2 * seq + head
-    ids = lax.dynamic_slice_in_dim(segment_ids, segment * rows, rows)
-    row_ids, col_ids = ids[:, None], ids[None, :]
-    first = (row_ids == ids[0]).astype(F32)
-    last = (row_ids == ids[rows - 1]).astype(F32)
-    table = jnp.asarray(feature_table())
 
     normed_one = rms_scale(inputs, gain_first).astype(BF)
     qkv = dot_nn(normed_one, qkv_full).astype(BF)
@@ -696,6 +1195,82 @@
     )
     residual = inputs + dot_nn(attended, out_full)
     normed_two = rms_scale(residual, gain_second).astype(BF)
+
+    return (
+        gate_w, up_w, down_w, qkv_full, out_full, gain_first, gain_second, normed_one,
+        query, keys, values, attended, rden, residual, normed_two, before,
+    )
+
+
+def body(
+    layer_input,
+    segment_ids,
+    norm1_gain,
+    w_query,
+    w_key,
+    w_value,
+    w_out,
+    norm2_gain,
+    w_gate,
+    w_up,
+    w_down,
+    output_grad,
+):
+    rows = layer_input.shape[1]
+    head, seq = lax.axis_index("head"), lax.axis_index("seq")
+    n_seq = lax.axis_size("seq")
+    qk = HEADS * QD
+    inputs = layer_input[0].astype(F32)
+    width = inputs.shape[1]
+
+    segment = 2 * seq + head
+    ids = lax.dynamic_slice_in_dim(segment_ids, segment * rows, rows)
+    row_ids, col_ids = ids[:, None], ids[None, :]
+    first = (row_ids == ids[0]).astype(F32)
+    last = (row_ids == ids[rows - 1]).astype(F32)
+    table = jnp.asarray(feature_table())
+    vcols = HEADS * VD
+    t_spec, q_spec = full_spec((8, FEATS)), full_spec((rows, qk))
+    one_spec, row_spec = full_spec((rows, 1)), full_spec((1, rows))
+    p_spec = pair_spec(rows)
+    f32_like = jax.ShapeDtypeStruct((rows, vcols), F32)
+    bf_like = jax.ShapeDtypeStruct((rows, vcols), BF)
+    slot = head * n_seq + seq
+    small = norm1_gain.shape[0]
+
+    if n_seq == 16:
+        gain_cols = jnp.stack([norm1_gain, norm2_gain], axis=1)
+        gain_cols = jnp.pad(gain_cols, ((0, 0), (0, GAIN_COLS - 2)))
+        (
+            g_own, g_other, u_own, u_other, d_own, d_other, wq, wo, qkv, attended, rden,
+            residual, normed_two, wide, thin, gains,
+        ) = forward(
+            layer_input[0],
+            jnp.concatenate([w_query, w_key, w_value, gain_cols], axis=1),
+            w_out,
+            [w_gate, w_up, w_down.T],
+            row_ids, col_ids, first, last, table, exchange_gates(segment_ids, rows, True),
+        )
+
+        def flat(weight):
+            return weight.reshape(-1, weight.shape[-1])
+
+        gate_w, up_w, down_w = (
+            [flat(g_own), flat(g_other)], [flat(u_own), flat(u_other)], [flat(d_own), flat(d_other)],
+        )
+        qkv_full, out_full = flat(wq)[:, : 2 * qk + vcols], flat(wo)
+        gain_first, gain_second = gains[0], gains[1]
+        normed_one = rms_scale(inputs, gain_first).astype(BF)
+        query, keys, values = qkv[:, :qk], qkv[:, qk : 2 * qk], qkv[:, 2 * qk :]
+        before = (wide, thin)
+    else:
+        (
+            gate_w, up_w, down_w, qkv_full, out_full, gain_first, gain_second, normed_one,
+            query, keys, values, attended, rden, residual, normed_two, before,
+        ) = plain_forward(
+            inputs, segment_ids, norm1_gain, w_query, w_key, w_value, w_out, norm2_gain, w_gate,
+            w_up, w_down, row_ids, col_ids, first, last, table,
+        )
 
     grad_output = output_grad[0]
     outcome = residual

time: 641 us -> 545 us (0.85)
  waiting for transfers between devices: 224 us -> 121 us
  Pallas kernels: 96.8 us -> 176 us
  starting transfers between devices: 116 us -> 58.7 us
  matrix products: 87.6 us -> 79 us
    pallas_call x8 -> x1, Pallas kernels: 25.7 us -> 127 us  [forward(): pl.pallas_call(forward_kernel, out_shape=out_shape, in_specs=[vmem] * 11...]
    ppermute x84 -> x38, waiting for transfers between devices: 122 us -> 55.8 us  [flip_seq(): return lax.ppermute(value, 'seq', [(i, i ^ code) for i in range(n)])]
    ppermute x20 -> x8, waiting for transfers between devices: 81 us -> 55.8 us  [flip_head(): return lax.ppermute(value, 'head', [(i, i ^ 1) for i in range(n)])]
    ppermute x84 -> x38, starting transfers between devices: 68.9 us -> 44.9 us  [flip_seq(): return lax.ppermute(value, 'seq', [(i, i ^ code) for i in range(n)])]
    pallas_call x6 -> x3, Pallas kernels: 71.1 us -> 48.6 us  [run(): pl.pallas_call(kernel, grid=(PAIRS,), in_specs=in_specs, out_specs=out_sp...]
    ppermute x8 -> x4, starting transfers between devices: 24.8 us -> 5.17 us  [shift_seq(): lax.ppermute(value, 'seq', [(i, i + distance) for i in range(n) if 0 <= i...]
    ppermute x20 -> x8, starting transfers between devices: 22.2 us -> 8.67 us  [flip_head(): return lax.ppermute(value, 'head', [(i, i ^ 1) for i in range(n)])]
    ppermute x8 -> x4, waiting for transfers between devices: 20.9 us -> 9.06 us  [shift_seq(): lax.ppermute(value, 'seq', [(i, i + distance) for i in range(n) if 0 <= i...]
  transfers between devices with their start and end apart: 112 -> 50, of which waited for: 37 -> 19; matrix products, arithmetic and copies ran while one was open for 17% -> 20% of each run, Pallas kernels for 8% -> 8%
where the time goes in v2:
time: 545 us; the launch traced here: 537 us
  Pallas kernels  176 us (32%)
  waiting for transfers between devices  121 us (22%)
  matrix products  79 us (14%)
  starting transfers between devices  58.7 us (11%)
  local copies, waits for them, and re-layouts  47.1 us (9%)
  other arithmetic  39.4 us (7%)
  between operations  16.8 us (3%)
    pallas_call x1, Pallas kernels, forward(): pl.pallas_call(forward_kernel, out_shape=out_shape, in_specs=[vmem] * 11...  127 us
    ppermute x8, waiting for transfers between devices, flip_head(): return lax.ppermute(value, 'head', [(i, i ^ 1) for i in range(n)])  55.8 us
    ppermute x38, waiting for transfers between devices, flip_seq(): return lax.ppermute(value, 'seq', [(i, i ^ code) for i in range(n)])  55.8 us
    pallas_call x3, Pallas kernels, run(): pl.pallas_call(kernel, grid=(PAIRS,), in_specs=in_specs, out_specs=out_sp...  48.6 us
    ppermute x38, starting transfers between devices, flip_seq(): return lax.ppermute(value, 'seq', [(i, i ^ code) for i in range(n)])  44.9 us
    dot_general x20, matrix products, dot_tn(): lax.dot_general(a, b, (((0,), (0,)), ((), ())), preferred_element_type=F32)  42.6 us
    dot_general x6, matrix products, dot_nn(): return jnp.dot(a, b, preferred_element_type=F32)  20.4 us
    dot_general x8, matrix products, dot_nt(): lax.dot_general(a, b, (((1,), (1,)), ((), ())), preferred_element_type=F32)  16 us
  transfers between devices with their start and end apart: 50, of which 19 were waited for; matrix products, arithmetic and copies ran while one was open for 20% of the time, Pallas kernels for 8%

profile of v2, /device:TPU:0, one launch (start us, length us, event | category | flops | bytes accessed | tf_op | source)
XLA Modules:
  0.0 537.4 jit_solution(17947837295118380221)
XLA Ops:
  20.9 127.1 %forward.1 = (bf16[4,2,2,64,1376]{4,3,2,1,0:T(8,128)(2,1)}, bf16[4,2,2,64,1376]{4,3,2,1,0:T(8,128)(2,1)}, bf16[4,2,2,64,1376]{4,3,2,1,0:T(8,128)(2,1)}, bf16[4,2...) custom-call(bf16[512,1024]{1,0:T(8,128)(2,1)} %bitcast.269, ...), custom_call_target="tpu_custom_call" | custom-call | flops 8589934592 | bytes 67108864 | tf_op jit(solution)/shard_map/forward/pallas_call | solution.py:1088
  148.0 4.0 fusion.80
  152.0 3.3 fusion.81
  162.2 5.4 %multiply_convert_fusion = (bf16[512,1376]{0,1:T(8,128)(2,1)S(1)}, bf16[512,1376]{0,1:T(8,128)(2,1)S(1)}, bf16[512,1376]{0,1:T(8,128)(2,1)}) fusion(f32[512,1376]{0,1:T(8,128)S(1)} %fusion.80, f32[512,1376]{0,1:T(8,128)} %fusion.81, bf16[1024,1376]{1,0:T(8,128)(2,1)S(1)} %bitcast.321, bf16[1,512,1024]{2,1,0:T(8,128)(2,1)S(1)} %copy-done.26), kind=kOutput, calls=%fused_computation.51 | convolution fusion | flops 1454112768 | bytes 13729792 | tf_op jit(solution)/shard_map/dot_general | solution.py:1111
  170.4 4.4 multiply_convert_fusion.1
  185.5 7.8 %grad_state_kernel.1 = (bf16[8,160,128]{2,1,0:T(8,128)(2,1)S(1)}, f32[8,8,160]{2,1,0:T(8,128)S(1)}) custom-call(f32[8,160]{1,0:T(8,128)S(1)} %copy-done.6, bf16[512,256]{1,0:T(8,128)(2,1)S(1)} %get-tuple-element.68.query_ref, bf16[512,1024]{1,0:T(8,128)(2,1)S(1)} %convolution_convert_fusion.16.grad_ref, bf16[512,1024]{1,0:T(8,128)(2,1)S(1)} %copy-done, ...), custom_call_target="tpu_custom_call" | custom-call | flops 2684354560 | bytes 4463616 | tf_op jit(solution)/shard_map/grad_state_kernel/pallas_call | solution.py:489
  218.7 2.6 fusion.4
  230.9 2.9 fusion.34
  235.3 29.3 %local_grad_kernel.1 = (bf16[512,256]{1,0:T(8,128)(2,1)S(1)}, f32[512,256]{1,0:T(8,128)S(1)}, f32[512,1024]{1,0:T(8,128)}) custom-call(f32[8,160]{1,0:T(8,128)S(1)} %copy-done.6, bf16[512,256]{1,0:T(8,128)(2,1)S(1)} %get-tuple-element.68.query_ref, bf16[512,256]{1,0:T(8,128)(2,1)S(1)} %get-tuple-element.67.keys_ref, bf16[512,1024]{1,0:T(8,128)(2,1)S(1)} %slice.92.values_ref, ...), custom_call_target="tpu_custom_call" | custom-call | flops 21474836480 | bytes 6147072 | tf_op jit(solution)/shard_map/local_grad_kernel/pallas_call | solution.py:489
  293.4 5.7 %collective-permute-done.3 = bf16[4,160,128]{2,1,0:T(8,128)(2,1)S(1)} collective-permute-done((bf16[4,160,128]{2,1,0:T(8,128)(2,1)S(1)}, bf16[4,160,128]{2,1,0:T(8,128)(2,1)S(1)}, u32[]{:S(2)}, u32[]{:S(2)}) %collective-permute-start.3) | collective-permute-done | bytes 163872 | tf_op jit(solution)/shard_map/ppermute | solution.py:37
  304.0 11.4 %finish_grad_kernel.1 = (bf16[512,256]{1,0:T(8,128)(2,1)S(1)}, bf16[512,1024]{1,0:T(8,128)(2,1)S(1)}) custom-call(f32[8,160]{1,0:T(8,128)S(1)} %copy-done.6, bf16[512,256]{1,0:T(8,128)(2,1)S(1)} %get-tuple-element.67.keys_ref, bf16[512,1024]{1,0:T(8,128)(2,1)S(1)} %slice.92.values_ref, f32[512,256]{1,0:T(8,128)S(1)} %copy-done.12, ...), custom_call_target="tpu_custom_call" | custom-call | flops 5368709120 | bytes 4307968 | tf_op jit(solution)/shard_map/finish_grad_kernel/pallas_call | solution.py:489
  325.0 3.7 collective-permute-start.12
  337.7 4.8 collective-permute-done.25
  342.7 2.7 collective-permute-start.28
  354.6 3.9 add_convert_fusion.6
  358.5 3.5 add_convert_fusion.1
  365.6 3.5 add_convert_fusion
  373.8 3.4 add_convert_fusion.3
  378.4 34.5 %collective-permute-done.17 = bf16[256,1536]{1,0:T(8,128)(2,1)} collective-permute-done((bf16[256,1536]{1,0:T(8,128)(2,1)}, bf16[256,1536]{1,0:T(8,128)(2,1)}, u32[]{:S(2)}, u32[]{:S(2)}) %collective-permute-start.17) | collective-permute-done | bytes 786464 | tf_op jit(solution)/shard_map/ppermute | solution.py:32
  417.6 3.5 add_convert_fusion.5
  427.1 15.5 %collective-permute-done.38 = bf16[512,1376]{0,1:T(8,128)(2,1)} collective-permute-done((bf16[512,1376]{0,1:T(8,128)(2,1)}, bf16[512,1376]{0,1:T(8,128)(2,1)}, u32[]{:S(2)}, u32[]{:S(2)}) %collective-permute-start.38) | collective-permute-done | bytes 1409056 | tf_op jit(solution)/shard_map/ppermute | solution.py:32
  442.6 4.3 add_convert_fusion.2
  457.3 3.2 collective-permute-start.21
  467.0 12.1 %collective-permute-done.20 = bf16[32,1536]{1,0:T(8,128)(2,1)S(1)} collective-permute-done((bf16[32,1536]{1,0:T(8,128)(2,1)S(1)}, bf16[32,1536]{1,0:T(8,128)(2,1)S(1)}, u32[]{:S(2)}, u32[]{:S(2)}) %collective-permute-start.20) | collective-permute-done | bytes 98336 | tf_op jit(solution)/shard_map/ppermute | solution.py:27
  479.2 3.8 collective-permute-start.46
  483.6 13.5 %collective-permute-done.47 = bf16[2,64,1376]{2,1,0:T(8,128)(2,1)S(1)} collective-permute-done((bf16[2,64,1376]{2,1,0:T(8,128)(2,1)S(1)}, bf16[2,64,1376]{2,1,0:T(8,128)(2,1)S(1)}, u32[]{:S(2)}, u32[]{:S(2)}) %collective-permute-start.47) | collective-permute-done | bytes 352288 | tf_op jit(solution)/shard_map/ppermute | solution.py:27
  499.3 3.7 collective-permute-done.49
  505.1 2.7 collective-permute-start.35
  509.8 2.7 collective-permute-start.42
  514.4 8.2 %collective-permute-start.40 = (bf16[64,1376]{1,0:T(8,128)(2,1)S(1)}, bf16[64,1376]{1,0:T(8,128)(2,1)S(1)}, u32[]{:S(2)}, u32[]{:S(2)}) collective-permute-start(bf16[64,1376]{1,0:T(8,128)(2,1)S(1)} %get-tuple-element.84), channel_id=1, source_target_pairs={{0,4},{1,5},{2,6},{3,7},{4,0},{5,1},{6,2},{7,3},{8,12},{9,13},{10,... | collective-permute-start | bytes 528392 | tf_op jit(solution)/shard_map/ppermute | solution.py:27
  522.6 7.7 %collective-permute-done.34 = bf16[64,1376]{1,0:T(8,128)(2,1)S(1)} collective-permute-done((bf16[64,1376]{1,0:T(8,128)(2,1)S(1)}, bf16[64,1376]{1,0:T(8,128)(2,1)S(1)}, u32[]{:S(2)}, u32[]{:S(2)}) %collective-permute-start.34) | collective-permute-done | bytes 176160 | tf_op jit(solution)/shard_map/ppermute | solution.py:27
  531.2 5.0 collective-permute-done.41
  (354 shorter events, 171.0 us)
Async XLA Ops:
  193.3 87.3 %collective-permute-start = (bf16[8,160,128]{2,1,0:T(8,128)(2,1)S(1)}, bf16[8,160,128]{2,1,0:T(8,128)(2,1)}, u32[]{:S(2)}, u32[]{:S(2)}) collective-permute-start(bf16[8,160,128]{2,1,0:T(8,128)(2,1)S(1)} %get-tuple-element.52), channel_id=1, source_target_pairs={{0,16},{16,0},{1,17},{17,1},{2,18},{18,2},{3,19},{19,3},{4,20},{20... | collective-permute-start | bytes 983048 | tf_op jit(solution)/shard_map/ppermute | solution.py:32
  193.4 75.6 %collective-permute-start.5 = (f32[8,8,160]{2,1,0:T(8,128)S(1)}, f32[8,8,160]{2,1,0:T(8,128)}, u32[]{:S(2)}, u32[]{:S(2)}) collective-permute-start(f32[8,8,160]{2,1,0:T(8,128)S(1)} %get-tuple-element.53), channel_id=1, source_target_pairs={{0,16},{16,0},{1,17},{17,1},{2,18},{18,2},{3,19},{19,3},{4,20},{20... | collective-permute-start | bytes 122888 | tf_op jit(solution)/shard_map/ppermute | solution.py:32
  200.0 100.3 %collective-permute-start.23 = (bf16[256,1024]{1,0:T(8,128)(2,1)}, bf16[256,1024]{1,0:T(8,128)(2,1)}, u32[]{:S(2)}, u32[]{:S(2)}) collective-permute-start(bf16[256,1024]{1,0:T(8,128)(2,1)} %convolution_convert_fusion.17), channel_id=1, source_target_pairs={{0,1},{1,0},{2,3},{3,2},{4,5},{5,4},{6,7},{7,6},{8,9},{9,8},{10,11... | collective-permute-start | bytes 1572872 | tf_op jit(solution)/shard_map/ppermute | solution.py:27
  201.3 129.5 %collective-permute-start.22 = (bf16[256,1024]{1,0:T(8,128)(2,1)}, bf16[256,1024]{1,0:T(8,128)(2,1)}, u32[]{:S(2)}, u32[]{:S(2)}) collective-permute-start(bf16[256,1024]{1,0:T(8,128)(2,1)} %convolution_convert_fusion.19), channel_id=1, source_target_pairs={{0,1},{1,0},{2,3},{3,2},{4,5},{5,4},{6,7},{7,6},{8,9},{9,8},{10,11... | collective-permute-start | bytes 1572872 | tf_op jit(solution)/shard_map/ppermute | solution.py:27
  278.7 75.3 %collective-permute-start.30 = (bf16[512,1376]{0,1:T(8,128)(2,1)}, bf16[512,1376]{0,1:T(8,128)(2,1)}, u32[]{:S(2)}, u32[]{:S(2)}) collective-permute-start(bf16[512,1376]{0,1:T(8,128)(2,1)} %convolution_convert_fusion.8), channel_id=1, source_target_pairs={{0,1},{1,0},{2,3},{3,2},{4,5},{5,4},{6,7},{7,6},{8,9},{9,8},{10,11... | collective-permute-start | bytes 4227080 | tf_op jit(solution)/shard_map/ppermute | solution.py:27
  290.0 9.2 %collective-permute-start.3 = (bf16[4,160,128]{2,1,0:T(8,128)(2,1)S(1)}, bf16[4,160,128]{2,1,0:T(8,128)(2,1)S(1)}, u32[]{:S(2)}, u32[]{:S(2)}) collective-permute-start(bf16[4,160,128]{2,1,0:T(8,128)(2,1)S(1)} %fusion.55), channel_id=1, source_target_pairs={{4,0},{5,1},{6,2},{7,3},{8,4},{9,5},{10,6},{11,7},{12,8},{13,9},{1... | collective-permute-start | bytes 491528 | tf_op jit(solution)/shard_map/ppermute | solution.py:37
  299.1 59.3 %collective-permute-start.43 = (bf16[512,1376]{0,1:T(8,128)(2,1)}, bf16[512,1376]{0,1:T(8,128)(2,1)}, u32[]{:S(2)}, u32[]{:S(2)}) collective-permute-start(bf16[512,1376]{0,1:T(8,128)(2,1)} %convolution_convert_fusion.2), channel_id=1, source_target_pairs={{0,1},{1,0},{2,3},{3,2},{4,5},{5,4},{6,7},{7,6},{8,9},{9,8},{10,11... | collective-permute-start | bytes 4227080 | tf_op jit(solution)/shard_map/ppermute | solution.py:27
  302.1 30.6 %collective-permute-start.24 = (bf16[256,1024]{1,0:T(8,128)(2,1)S(1)}, bf16[256,1024]{1,0:T(8,128)(2,1)S(1)}, u32[]{:S(2)}, u32[]{:S(2)}) collective-permute-start(bf16[256,1024]{1,0:T(8,128)(2,1)S(1)} %add_convert_fusion.13), channel_id=1, source_target_pairs={{0,16},{16,0},{1,17},{17,1},{2,18},{18,2},{3,19},{19,3},{4,20},{20... | collective-permute-start | bytes 1572872 | tf_op jit(solution)/shard_map/ppermute | solution.py:32
  330.5 34.2 %collective-permute-start.44 = (bf16[512,1376]{0,1:T(8,128)(2,1)}, bf16[512,1376]{0,1:T(8,128)(2,1)}, u32[]{:S(2)}, u32[]{:S(2)}) collective-permute-start(bf16[512,1376]{0,1:T(8,128)(2,1)} %convolution_convert_fusion), channel_id=1, source_target_pairs={{0,1},{1,0},{2,3},{3,2},{4,5},{5,4},{6,7},{7,6},{8,9},{9,8},{10,11... | collective-permute-start | bytes 4227080 | tf_op jit(solution)/shard_map/ppermute | solution.py:27
  336.5 10.4 %collective-permute-start.14 = (f32[2,1024]{1,0:T(2,128)S(1)}, f32[2,1024]{1,0:T(2,128)S(1)}, u32[]{:S(2)}, u32[]{:S(2)}) collective-permute-start(f32[2,1024]{1,0:T(2,128)S(1)} %add.439), channel_id=1, source_target_pairs={{0,8},{1,9},{2,10},{3,11},{4,12},{5,13},{6,14},{7,15},{8,0},{9,1},... | collective-permute-start | bytes 24584 | tf_op jit(solution)/shard_map/ppermute | solution.py:27
  352.2 64.8 %collective-permute-start.29 = (bf16[512,1376]{0,1:T(8,128)(2,1)}, bf16[512,1376]{0,1:T(8,128)(2,1)}, u32[]{:S(2)}, u32[]{:S(2)}) collective-permute-start(bf16[512,1376]{0,1:T(8,128)(2,1)} %convolution_convert_fusion.10), channel_id=1, source_target_pairs={{0,1},{1,0},{2,3},{3,2},{4,5},{5,4},{6,7},{7,6},{8,9},{9,8},{10,11... | collective-permute-start | bytes 4227080 | tf_op jit(solution)/shard_map/ppermute | solution.py:27
  354.1 19.2 %collective-permute-start.37 = (bf16[512,1376]{0,1:T(8,128)(2,1)}, bf16[512,1376]{0,1:T(8,128)(2,1)}, u32[]{:S(2)}, u32[]{:S(2)}) collective-permute-start(bf16[512,1376]{0,1:T(8,128)(2,1)} %convolution_convert_fusion.4), channel_id=1, source_target_pairs={{0,1},{1,0},{2,3},{3,2},{4,5},{5,4},{6,7},{7,6},{8,9},{9,8},{10,11... | collective-permute-start | bytes 4227080 | tf_op jit(solution)/shard_map/ppermute | solution.py:27
  358.4 18.8 %collective-permute-start.15 = (bf16[256,1536]{1,0:T(8,128)(2,1)}, bf16[256,1536]{1,0:T(8,128)(2,1)}, u32[]{:S(2)}, u32[]{:S(2)}) collective-permute-start(bf16[256,1536]{1,0:T(8,128)(2,1)} %convolution_convert_fusion.14), channel_id=1, source_target_pairs={{0,1},{1,0},{2,3},{3,2},{4,5},{5,4},{6,7},{7,6},{8,9},{9,8},{10,11... | collective-permute-start | bytes 2359304 | tf_op jit(solution)/shard_map/ppermute | solution.py:27
  362.0 55.6 %collective-permute-start.31 = (bf16[512,1376]{0,1:T(8,128)(2,1)}, bf16[512,1376]{0,1:T(8,128)(2,1)}, u32[]{:S(2)}, u32[]{:S(2)}) collective-permute-start(bf16[512,1376]{0,1:T(8,128)(2,1)} %add_convert_fusion.6), channel_id=1, source_target_pairs={{0,16},{16,0},{1,17},{17,1},{2,18},{18,2},{3,19},{19,3},{4,20},{20... | collective-permute-start | bytes 4227080 | tf_op jit(solution)/shard_map/ppermute | solution.py:32
  364.7 48.2 %collective-permute-start.17 = (bf16[256,1536]{1,0:T(8,128)(2,1)}, bf16[256,1536]{1,0:T(8,128)(2,1)}, u32[]{:S(2)}, u32[]{:S(2)}) collective-permute-start(bf16[256,1536]{1,0:T(8,128)(2,1)} %add_convert_fusion.10), channel_id=1, source_target_pairs={{0,16},{16,0},{1,17},{17,1},{2,18},{18,2},{3,19},{19,3},{4,20},{20... | collective-permute-start | bytes 2359304 | tf_op jit(solution)/shard_map/ppermute | solution.py:32
  373.2 53.9 %collective-permute-start.36 = (bf16[512,1376]{0,1:T(8,128)(2,1)}, bf16[512,1376]{0,1:T(8,128)(2,1)}, u32[]{:S(2)}, u32[]{:S(2)}) collective-permute-start(bf16[512,1376]{0,1:T(8,128)(2,1)} %convolution_convert_fusion.6), channel_id=1, source_target_pairs={{0,1},{1,0},{2,3},{3,2},{4,5},{5,4},{6,7},{7,6},{8,9},{9,8},{10,11... | collective-permute-start | bytes 4227080 | tf_op jit(solution)/shard_map/ppermute | solution.py:27
  377.2 65.4 %collective-permute-start.38 = (bf16[512,1376]{0,1:T(8,128)(2,1)}, bf16[512,1376]{0,1:T(8,128)(2,1)}, u32[]{:S(2)}, u32[]{:S(2)}) collective-permute-start(bf16[512,1376]{0,1:T(8,128)(2,1)} %add_convert_fusion.3), channel_id=1, source_target_pairs={{0,16},{16,0},{1,17},{17,1},{2,18},{18,2},{3,19},{19,3},{4,20},{20... | collective-permute-start | bytes 4227080 | tf_op jit(solution)/shard_map/ppermute | solution.py:32
  412.9 39.3 %collective-permute-start.45 = (bf16[4,2,64,1376]{3,2,0,1:T(8,128)(2,1)}, bf16[4,2,64,1376]{3,2,0,1:T(8,128)(2,1)}, u32[]{:S(2)}, u32[]{:S(2)}) collective-permute-start(bf16[4,2,64,1376]{3,2,0,1:T(8,128)(2,1)} %fusion.29), channel_id=1, source_target_pairs={{0,2},{1,3},{2,0},{3,1},{4,6},{5,7},{6,4},{7,5},{8,10},{9,11},{10,... | collective-permute-start | bytes 4227080 | tf_op jit(solution)/shard_map/ppermute | solution.py:27
  417.0 39.1 %collective-permute-start.18 = (bf16[4,32,1536]{2,1,0:T(8,128)(2,1)S(1)}, bf16[4,32,1536]{2,1,0:T(8,128)(2,1)}, u32[]{:S(2)}, u32[]{:S(2)}) collective-permute-start(bf16[4,32,1536]{2,1,0:T(8,128)(2,1)S(1)} %dynamic-slice_bitcast_fusion.2), channel_id=1, source_target_pairs={{0,2},{1,3},{2,0},{3,1},{4,6},{5,7},{6,4},{7,5},{8,10},{9,11},{10,... | collective-permute-start | bytes 1179656 | tf_op jit(solution)/shard_map/ppermute | solution.py:27
  425.6 78.1 %collective-permute-start.32 = (bf16[4,64,1376]{2,1,0:T(8,128)(2,1)}, bf16[4,64,1376]{2,1,0:T(8,128)(2,1)}, u32[]{:S(2)}, u32[]{:S(2)}) collective-permute-start(bf16[4,64,1376]{2,1,0:T(8,128)(2,1)} %dynamic-slice_bitcast_fusion.1), channel_id=1, source_target_pairs={{0,2},{1,3},{2,0},{3,1},{4,6},{5,7},{6,4},{7,5},{8,10},{9,11},{10,... | collective-permute-start | bytes 2113544 | tf_op jit(solution)/shard_map/ppermute | solution.py:27
  450.6 58.9 %collective-permute-start.39 = (bf16[4,64,1376]{2,1,0:T(8,128)(2,1)S(1)}, bf16[4,64,1376]{2,1,0:T(8,128)(2,1)S(1)}, u32[]{:S(2)}, u32[]{:S(2)}) collective-permute-start(bf16[4,64,1376]{2,1,0:T(8,128)(2,1)S(1)} %dynamic-slice_bitcast_fusion), channel_id=1, source_target_pairs={{0,2},{1,3},{2,0},{3,1},{4,6},{5,7},{6,4},{7,5},{8,10},{9,11},{10,... | collective-permute-start | bytes 2113544 | tf_op jit(solution)/shard_map/ppermute | solution.py:27
  460.4 18.7 %collective-permute-start.20 = (bf16[32,1536]{1,0:T(8,128)(2,1)S(1)}, bf16[32,1536]{1,0:T(8,128)(2,1)S(1)}, u32[]{:S(2)}, u32[]{:S(2)}) collective-permute-start(bf16[32,1536]{1,0:T(8,128)(2,1)S(1)} %get-tuple-element.92), channel_id=1, source_target_pairs={{0,8},{1,9},{2,10},{3,11},{4,12},{5,13},{6,14},{7,15},{8,0},{9,1},... | collective-permute-start | bytes 294920 | tf_op jit(solution)/shard_map/ppermute | solution.py:27
  460.4 18.7 %collective-permute-start.19 = (bf16[32,1536]{1,0:T(8,128)(2,1)S(1)}, bf16[32,1536]{1,0:T(8,128)(2,1)S(1)}, u32[]{:S(2)}, u32[]{:S(2)}) collective-permute-start(bf16[32,1536]{1,0:T(8,128)(2,1)S(1)} %get-tuple-element.90), channel_id=1, source_target_pairs={{0,4},{1,5},{2,6},{3,7},{4,0},{5,1},{6,2},{7,3},{8,12},{9,13},{10,... | collective-permute-start | bytes 294920 | tf_op jit(solution)/shard_map/ppermute | solution.py:27
  464.4 19.2 %collective-permute-start.48 = (bf16[2,64,1376]{2,1,0:T(8,128)(2,1)S(1)}, bf16[2,64,1376]{2,1,0:T(8,128)(2,1)S(1)}, u32[]{:S(2)}, u32[]{:S(2)}) collective-permute-start(bf16[2,64,1376]{2,1,0:T(8,128)(2,1)S(1)} %get-tuple-element.70), channel_id=1, source_target_pairs={{0,12},{1,13},{2,14},{3,15},{4,8},{5,9},{6,10},{7,11},{8,4},{9,5},... | collective-permute-start | bytes 1056776 | tf_op jit(solution)/shard_map/ppermute | solution.py:27
  479.2 18.0 %collective-permute-start.47 = (bf16[2,64,1376]{2,1,0:T(8,128)(2,1)S(1)}, bf16[2,64,1376]{2,1,0:T(8,128)(2,1)S(1)}, u32[]{:S(2)}, u32[]{:S(2)}) collective-permute-start(bf16[2,64,1376]{2,1,0:T(8,128)(2,1)S(1)} %get-tuple-element.71), channel_id=1, source_target_pairs={{0,8},{1,9},{2,10},{3,11},{4,12},{5,13},{6,14},{7,15},{8,0},{9,1},... | collective-permute-start | bytes 1056776 | tf_op jit(solution)/shard_map/ppermute | solution.py:27
  479.2 18.0 %collective-permute-start.46 = (bf16[2,64,1376]{2,1,0:T(8,128)(2,1)S(1)}, bf16[2,64,1376]{2,1,0:T(8,128)(2,1)S(1)}, u32[]{:S(2)}, u32[]{:S(2)}) collective-permute-start(bf16[2,64,1376]{2,1,0:T(8,128)(2,1)S(1)} %get-tuple-element.69), channel_id=1, source_target_pairs={{0,4},{1,5},{2,6},{3,7},{4,0},{5,1},{6,2},{7,3},{8,12},{9,13},{10,... | collective-permute-start | bytes 1056776 | tf_op jit(solution)/shard_map/ppermute | solution.py:27
  505.1 9.4 %collective-permute-start.35 = (bf16[64,1376]{1,0:T(8,128)(2,1)S(1)}, bf16[64,1376]{1,0:T(8,128)(2,1)S(1)}, u32[]{:S(2)}, u32[]{:S(2)}) collective-permute-start(bf16[64,1376]{1,0:T(8,128)(2,1)S(1)} %get-tuple-element.88), channel_id=1, source_target_pairs={{0,12},{1,13},{2,14},{3,15},{4,8},{5,9},{6,10},{7,11},{8,4},{9,5},... | collective-permute-start | bytes 528392 | tf_op jit(solution)/shard_map/ppermute | solution.py:27
  507.8 22.6 %collective-permute-start.34 = (bf16[64,1376]{1,0:T(8,128)(2,1)S(1)}, bf16[64,1376]{1,0:T(8,128)(2,1)S(1)}, u32[]{:S(2)}, u32[]{:S(2)}) collective-permute-start(bf16[64,1376]{1,0:T(8,128)(2,1)S(1)} %get-tuple-element.89), channel_id=1, source_target_pairs={{0,8},{1,9},{2,10},{3,11},{4,12},{5,13},{6,14},{7,15},{8,0},{9,1},... | collective-permute-start | bytes 528392 | tf_op jit(solution)/shard_map/ppermute | solution.py:27
  507.8 22.6 %collective-permute-start.33 = (bf16[64,1376]{1,0:T(8,128)(2,1)S(1)}, bf16[64,1376]{1,0:T(8,128)(2,1)S(1)}, u32[]{:S(2)}, u32[]{:S(2)}) collective-permute-start(bf16[64,1376]{1,0:T(8,128)(2,1)S(1)} %get-tuple-element.87), channel_id=1, source_target_pairs={{0,4},{1,5},{2,6},{3,7},{4,0},{5,1},{6,2},{7,3},{8,12},{9,13},{10,... | collective-permute-start | bytes 528392 | tf_op jit(solution)/shard_map/ppermute | solution.py:27
  509.8 21.4 %collective-permute-start.42 = (bf16[64,1376]{1,0:T(8,128)(2,1)S(1)}, bf16[64,1376]{1,0:T(8,128)(2,1)S(1)}, u32[]{:S(2)}, u32[]{:S(2)}) collective-permute-start(bf16[64,1376]{1,0:T(8,128)(2,1)S(1)} %get-tuple-element.85), channel_id=1, source_target_pairs={{0,12},{1,13},{2,14},{3,15},{4,8},{5,9},{6,10},{7,11},{8,4},{9,5},... | collective-permute-start | bytes 528392 | tf_op jit(solution)/shard_map/ppermute | solution.py:27
  512.5 23.6 %collective-permute-start.41 = (bf16[64,1376]{1,0:T(8,128)(2,1)S(1)}, bf16[64,1376]{1,0:T(8,128)(2,1)S(1)}, u32[]{:S(2)}, u32[]{:S(2)}) collective-permute-start(bf16[64,1376]{1,0:T(8,128)(2,1)S(1)} %get-tuple-element.86), channel_id=1, source_target_pairs={{0,8},{1,9},{2,10},{3,11},{4,12},{5,13},{6,14},{7,15},{8,0},{9,1},... | collective-permute-start | bytes 528392 | tf_op jit(solution)/shard_map/ppermute | solution.py:27
  514.4 21.7 %collective-permute-start.40 = (bf16[64,1376]{1,0:T(8,128)(2,1)S(1)}, bf16[64,1376]{1,0:T(8,128)(2,1)S(1)}, u32[]{:S(2)}, u32[]{:S(2)}) collective-permute-start(bf16[64,1376]{1,0:T(8,128)(2,1)S(1)} %get-tuple-element.84), channel_id=1, source_target_pairs={{0,4},{1,5},{2,6},{3,7},{4,0},{5,1},{6,2},{7,3},{8,12},{9,13},{10,... | collective-permute-start | bytes 528392 | tf_op jit(solution)/shard_map/ppermute | solution.py:27
  (95 other events, 601.8 us)
